TPU v7x, 32 devices: a whole 2x2x4 slice. The times are simulated.
32 devices in a mesh: groups: 2 (over x), ep: 16 (over z, y, core).
Axes of the slice: x: 2, y: 2, z: 4, core: 2. Of those that a mesh axis runs over, the one named last changes fastest.
Arguments:
- thinker_rows: bfloat16 [512, 2048], P(('groups', 'ep')), parts along dimension 0, may hold values from -6 to 6
- expert_ids: int32 [512, 8], P(('groups', 'ep')), parts along dimension 0, may hold values from 0 to 15, all different within a row; in each aligned block of 16 rows (0 to 15, 16 to 31, ...) at most 16 rows name the same one
- gate_weights: float32 [512, 8], P(('groups', 'ep')), parts along dimension 0, may hold values from 0.2 to 1
- w_gate: bfloat16 [16, 2048, 512], P('ep'), may hold values from -0.125 to 0.125
- w_up: bfloat16 [16, 2048, 512], P('ep'), may hold values from -0.125 to 0.125
- w_down: bfloat16 [16, 512, 2048], P('ep'), may hold values from -0.25 to 0.25
- talker_proj: bfloat16 [2048, 1024], replicated, may hold values from -0.125 to 0.125
- talker_slot: int32 [32, 16], P(('groups', 'ep')), parts along dimension 0, may hold values from 0 to 15, each once within a row
- speech_count: int32 [512], P(('groups', 'ep')), parts along dimension 0, may hold values from 0 to 4
- left_context: bfloat16 [512, 6, 1024], P(('groups', 'ep')), parts along dimension 0, may hold values from -6 to 6
- frame_offset: float32 [4, 1024], replicated, may hold values from -6 to 6
- conv_weight: float32 [7, 1024], replicated, may hold values from -2.4 to 2.4
Outputs:
- voice_frames: bfloat16 [512, 4, 1024], P(('groups', 'ep')), parts along dimension 0
There are 2 independent parts, one for each index of `groups`. A program takes and returns all parts, laid end to end along the dimension named above; an argument that names none is the same for every part. Nothing has to cross between parts.
Inputs may be any that keep to these rules, and one draw needn't show every extreme that they name: `expert_ids`: each row names 8 different experts; among the rows of one device no expert is named by more than 16 rows, and in every draw some expert is named by exactly 16 rows of some device. `talker_slot`: each device's row is a permutation of 0 to 15.
All inputs are finite; a program needn't handle non-finite values.
Results may differ from a plain program's by a relative error of at most 0.007.
Values may be sent and summed in bfloat16 or wider, within the bound.
No kernel may reach another device: no remote copies, remote signals or barrier semaphores. Data moves between devices by JAX's collectives and lax.ppermute only.
A program may use at most 64 MiB of HBM per device.

v0:
```python
import functools

import jax
import jax.numpy as jnp
import numpy as np
from jax import lax
from jax.experimental import pallas as pl
from jax.experimental.pallas import tpu as pltpu
from jax.sharding import PartitionSpec as P


CAP = 16
LANES = 128


def expert_block(block_rows, gate_mat, up_mat, down_mat):
    gate_act = jnp.dot(block_rows, gate_mat, preferred_element_type=jnp.float32)
    up_act = jnp.dot(block_rows, up_mat, preferred_element_type=jnp.float32)
    inner = (jax.nn.silu(gate_act) * up_act).astype(jnp.bfloat16)
    return jnp.dot(inner, down_mat, preferred_element_type=jnp.float32).astype(jnp.bfloat16)


def project(hidden, talker_proj):
    values = hidden.astype(jnp.float32)
    scaled = values * lax.rsqrt(jnp.mean(values * values, axis=-1, keepdims=True) + 1e-06)
    return jnp.dot(
        scaled.astype(jnp.bfloat16), talker_proj, preferred_element_type=jnp.float32
    ).astype(jnp.bfloat16)


def vocode(owned, speech_count, left_context, frame_offset, conv_weight):
    frames = owned.astype(jnp.float32)[:, None, :] + frame_offset[None, :, :]
    sequence = jnp.concatenate([left_context.astype(jnp.float32), frames], axis=1)
    taps = conv_weight.shape[0]
    horizon = frame_offset.shape[0]
    result = jnp.zeros_like(frames)
    for offset in range(taps):
        result = (
            result + conv_weight[offset][None, None, :] * sequence[:, offset : offset + horizon, :]
        )
    active = jnp.arange(horizon, dtype=jnp.int32)[None, :, None] < speech_count[:, None, None]
    return jnp.where(active, result, 0.0).astype(jnp.bfloat16)


def slot_positions(expert_ids, experts):
    flat_expert = expert_ids.reshape(-1)
    onehot = (flat_expert[:, None] == jnp.arange(experts, dtype=jnp.int32)[None, :]).astype(
        jnp.int32
    )
    position = jnp.sum((jnp.cumsum(onehot, axis=0) - onehot) * onehot, axis=1)
    return (flat_expert, position)


def run_and_return(buffer, w_gate, w_up, w_down):
    sources, slot_count, features = buffer.shape
    flattened = buffer.reshape(sources * slot_count, features)
    outputs = expert_block(flattened, w_gate[0], w_up[0], w_down[0]).reshape(
        sources, slot_count, features
    )
    return lax.all_to_all(outputs, "ep", split_axis=0, concat_axis=0, tiled=True)


def local_dispatch(
    thinker_rows,
    expert_ids,
    gate_weights,
    w_gate,
    w_up,
    w_down,
    talker_proj,
    talker_slot,
    speech_count,
    left_context,
    frame_offset,
    conv_weight,
):
    devices = lax.axis_size("ep")
    streams_here, features = thinker_rows.shape
    chosen = expert_ids.shape[1]
    flat_expert, position = slot_positions(expert_ids, devices)
    row_index = jnp.arange(streams_here * chosen, dtype=jnp.int32) // chosen
    outgoing = (
        jnp.zeros((devices, CAP, features), jnp.bfloat16)
        .at[flat_expert, position]
        .set(thinker_rows[row_index])
    )
    returned = run_and_return(
        lax.all_to_all(outgoing, "ep", split_axis=0, concat_axis=0, tiled=True),
        w_gate,
        w_up,
        w_down,
    )
    lookup = (
        returned[flat_expert, position].astype(jnp.float32).reshape(streams_here, chosen, features)
    )
    mixture = jnp.sum(gate_weights[:, :, None] * lookup, axis=1)
    hidden = (thinker_rows.astype(jnp.float32) + mixture).astype(jnp.bfloat16)
    slots = talker_slot[0]
    per_owner = streams_here // devices
    talker_rows = project(hidden, talker_proj)
    placed = (
        jnp.zeros_like(talker_rows)
        .at[slots]
        .set(talker_rows)
        .reshape(devices, per_owner, talker_rows.shape[1])
    )
    owned = lax.all_to_all(placed, "ep", split_axis=0, concat_axis=0, tiled=True).reshape(
        streams_here, talker_rows.shape[1]
    )
    return vocode(owned, speech_count, left_context, frame_offset, conv_weight)


def dot32(a, b):
    return jnp.dot(a, b, preferred_element_type=jnp.float32)


def sort_rows(experts, rows_ref, ids_ref, gates_ref, slot_ref, out_ref, at):
    rows, features = rows_ref.shape
    width = out_ref.shape[1] - features
    owner = lax.broadcasted_iota(jnp.int32, (rows, rows), 0)
    order = (owner == slot_ref[...]).astype(jnp.bfloat16)
    lane = lax.broadcasted_iota(jnp.int32, (width, rows), 0)
    expert = lane % experts
    gates = jnp.zeros((width, rows), jnp.float32)
    for j in range(ids_ref.shape[0]):
        gates = gates + jnp.where(expert == ids_ref[j : j + 1, :], gates_ref[j : j + 1, :], 0.0)
    high = gates.astype(jnp.bfloat16).astype(jnp.float32)
    middle = (gates - high).astype(jnp.bfloat16).astype(jnp.float32)
    low = gates - high - middle
    part = lane // experts
    packed = jnp.where(
        part == 0, high, jnp.where(part == 1, middle, jnp.where(part == 2, low, 0.0))
    ).astype(jnp.bfloat16)
    out_ref[at : at + rows, :features] = dot32(order, rows_ref[...]).astype(jnp.bfloat16)
    out_ref[at : at + rows, features:] = lax.dot_general(
        order, packed, (((1,), (1,)), ((), ())), preferred_element_type=jnp.float32
    ).astype(jnp.bfloat16)


def own_kernel(experts, rows_ref, ids_ref, gates_ref, slot_ref, out_ref):
    sort_rows(experts, rows_ref, ids_ref, gates_ref, slot_ref, out_ref, 0)


def pair_kernel(own_ref, other_ref, out_ref):
    rows = own_ref.shape[0]
    out_ref[:rows, :] = own_ref[...]
    out_ref[rows:, :] = other_ref[...]


def fetch_kernel(*refs):
    count = (len(refs) - 1) // 2
    sems = refs[-1]
    copies = [
        pltpu.make_async_copy(refs[i], refs[count + i], sems.at[i]) for i in range(count)
    ]
    for copy in copies:
        copy.start()
    for copy in copies:
        copy.wait()


def move_rows(me, rows, table_ref, target_ref):
    core = me % 2
    columns = table_ref.shape[1]
    origin = jnp.where(core == 0, table_ref[0:1, :], table_ref[1:2, :])
    owner = lax.broadcasted_iota(jnp.int32, (1, columns), 1) % rows
    target = jnp.where(core == 0, target_ref[:, 0:1], target_ref[:, 1:2])
    rank = lax.broadcasted_iota(jnp.int32, target.shape, 0) % rows
    hit = (origin == (target ^ rank)) & (owner == (target ^ me)) & (target >= 0)
    return jnp.where(hit, 1.0, 0.0).astype(jnp.bfloat16)


def activate(experts, parts, wg_ref, wu_ref, x_ref, inner_ref, first):
    me = lax.axis_index("ep")
    features, hidden = wg_ref.shape
    at = 0
    for part in parts:
        x_ref[at : at + part.shape[0], :] = part[...]
        at += part.shape[0]
    meta = x_ref[:, features:].astype(jnp.float32)
    lane = lax.broadcasted_iota(jnp.int32, (1, meta.shape[1]), 1)
    pick = (lane % experts == me) & (lane < 3 * experts)
    gate = jnp.sum(jnp.where(pick, meta, 0.0), axis=1, keepdims=True)
    step = min(256, hidden)
    for n in range(0, hidden, step):
        g = dot32(x_ref[:, :features], wg_ref[:, n : n + step])
        u = dot32(x_ref[:, :features], wu_ref[:, n : n + step])
        inner = (g * jax.nn.sigmoid(g) * u * gate).astype(jnp.bfloat16)
        inner_ref[first : first + at, n : n + step] = inner


def early_kernel(experts, wg_ref, wu_ref, *refs):
    activate(experts, refs[:-2], wg_ref, wu_ref, refs[-1], refs[-2], 0)


def late_kernel(experts, rows, table_ref, target_ref, wg_ref, wu_ref, wd_ref, early_ref, *refs):
    parts, (out_ref, inner_ref, x_ref) = refs[:-3], refs[-3:]
    first = early_ref.shape[0]
    inner_ref[:first, :] = early_ref[...]
    activate(experts, parts, wg_ref, wu_ref, x_ref, inner_ref, first)
    down_kernel(rows, table_ref, target_ref, wd_ref, inner_ref, out_ref)


def down_kernel(rows, table_ref, target_ref, wd_ref, inner_ref, *outs):
    me = lax.axis_index("ep")
    move = move_rows(me, rows, table_ref, target_ref)
    placed = dot32(move, inner_ref[...]).astype(jnp.bfloat16)
    features = wd_ref.shape[1]
    step = min(512, features)
    for n in range(0, features, step):
        y = dot32(placed, wd_ref[:, n : n + step]).astype(jnp.bfloat16)
        at = 0
        for out in outs:
            out[:, n : n + step] = y[at : at + out.shape[0]]
            at += out.shape[0]


def sum_kernel(ours_ref, given_ref, *outs):
    at = 0
    for out in outs:
        piece = slice(at, at + out.shape[0])
        total = ours_ref[piece, :].astype(jnp.float32) + given_ref[piece, :].astype(jnp.float32)
        out[...] = total.astype(jnp.bfloat16)
        at += out.shape[0]


def prepare_kernel(blocks, rows, table_ref, context_ref, offset_ref, conv_ref, *refs):
    parts, (rest_ref, base_ref, x_ref) = refs[:blocks], refs[blocks:]
    me = lax.axis_index("ep")
    features = rest_ref.shape[1]
    at = 0
    for part in parts:
        x_ref[at : at + part.shape[0], :] = part[:, :features]
        at += part.shape[0]
    columns = table_ref.shape[1]
    origin = jnp.where(me % 2 == 0, table_ref[0:1, :], table_ref[1:2, :])
    owner = lax.broadcasted_iota(jnp.int32, (1, columns), 1) % rows
    rank = lax.broadcasted_iota(jnp.int32, (rows, 1), 0)
    pick = jnp.where((origin == rank) & (owner == me), 1.0, 0.0).astype(jnp.bfloat16)
    rest_ref[...] = dot32(pick, x_ref[...]).astype(jnp.bfloat16)
    taps, horizon, past = conv_ref.shape[0], offset_ref.shape[0], context_ref.shape[0]
    context = [context_ref[i].astype(jnp.float32) for i in range(past)]
    for f in range(horizon):
        fixed = jnp.zeros((1, conv_ref.shape[1]), jnp.float32)
        for t in range(past - f, taps):
            i = f + t - past
            fixed = fixed + conv_ref[t : t + 1, :] * offset_ref[i : i + 1, :]
        total = jnp.broadcast_to(fixed, context[0].shape)
        for t in range(past - f):
            total = total + conv_ref[t : t + 1, :] * context[f + t]
        base_ref[:, f, :] = total


def owner_kernel(
    count_ref, mine_ref, got_ref, rest_ref, proj_ref, base_ref, conv_ref, out_ref
):
    me = lax.axis_index("ep")
    rows = rest_ref.shape[0]
    total = mine_ref[:rows, :] + got_ref[...].astype(jnp.float32)
    total = total + rest_ref[...].astype(jnp.float32)
    values = total.astype(jnp.bfloat16).astype(jnp.float32)
    normed = values * lax.rsqrt(jnp.mean(values * values, axis=-1, keepdims=True) + 1e-06)
    talker = dot32(normed.astype(jnp.bfloat16), proj_ref[...]).astype(jnp.bfloat16)
    one = lax.broadcasted_iota(jnp.int32, (rows, rows), 0)
    two = lax.broadcasted_iota(jnp.int32, (rows, rows), 1)
    order = jnp.where((one ^ two) == me, 1.0, 0.0).astype(jnp.bfloat16)
    owned = dot32(order, talker)
    taps, horizon = conv_ref.shape[0], base_ref.shape[1]
    frame = lax.broadcasted_iota(jnp.int32, (horizon, owned.shape[1]), 0)
    scale = jnp.zeros(frame.shape, jnp.float32)
    for t in range(taps):
        scale = scale + jnp.where(frame + t >= taps - 1, conv_ref[t : t + 1, :], 0.0)
    for q in range(rows):
        voice = base_ref[q] + scale * owned[q : q + 1, :]
        out_ref[q] = jnp.where(frame < count_ref[q], voice, 0.0).astype(jnp.bfloat16)


def vmem(count):
    return [pl.BlockSpec(memory_space=pltpu.VMEM)] * count


def gather_partners(chips):
    between = list(range(2, chips - 2))
    half = len(between) // 2
    return [
        [chips - 2, None] + between[:half],
        [chips - 1, 1] + between[half:],
    ]


def reduce_partners(chips):
    masks = list(range(chips - 1, 0, -1)) + [None]
    return [
        [m for k, m in enumerate(masks) if k % 4 in (0, 3)],
        [m for k, m in enumerate(masks) if k % 4 in (1, 2)],
    ]


def in_hbm(x):
    return pltpu.with_memory_space_constraint(x, pltpu.HBM)


def call(kernel, out_shape, operands, scalars=0, scratch=(), megabytes=4, cost=None, in_specs=None):
    several = isinstance(out_shape, (list, tuple))
    specs = [pl.BlockSpec(memory_space=pltpu.SMEM)] * scalars + vmem(len(operands) - scalars)
    return pl.pallas_call(
        kernel,
        out_shape=out_shape,
        in_specs=in_specs or specs,
        out_specs=vmem(len(out_shape)) if several else vmem(1)[0],
        scratch_shapes=list(scratch),
        compiler_params=pltpu.CompilerParams(vmem_limit_bytes=megabytes << 20),
        cost_estimate=cost,
    )(*operands)


def local_gather(
    thinker_rows,
    expert_ids,
    gate_weights,
    w_gate,
    w_up,
    w_down,
    talker_proj,
    talker_slot,
    speech_count,
    left_context,
    frame_offset,
    conv_weight,
):
    devices = lax.axis_size("ep")
    rows, features = thinker_rows.shape
    hidden = w_gate.shape[2]
    talker_width = talker_proj.shape[1]
    horizon = frame_offset.shape[0]
    lists = gather_partners(devices // 2)
    back = reduce_partners(devices // 2)
    slots = len(lists[0])
    width = -(-3 * devices // LANES) * LANES
    bf16 = functools.partial(jax.ShapeDtypeStruct, dtype=jnp.bfloat16)

    def far(x, chips, j):
        pairs = [(i, i ^ (chips[i % 2][j] * 2)) for i in range(devices) if chips[i % 2][j]]
        return lax.ppermute(x, "ep", pairs)

    def near(x, j=None):
        pairs = [(i, i ^ 1) for i in range(devices) if j is None or lists[i % 2][j]]
        return lax.ppermute(x, "ep", pairs)

    def side(chips, flip):
        blocks = [[-1, -1] if m is None else [2 * m + flip, 2 * m + 1 - flip] for m in chips]
        return [k for pair in blocks for k in pair]

    def spread(blocks):
        return np.repeat(np.array(blocks, np.int32), rows)

    first_slots, last_slots = range(slots // 2), range(slots // 2, slots)

    def arriving(c, chosen):
        some = [[chips[j] for j in chosen] for chips in (lists[c], lists[1 - c])]
        return side(some[0], 0) + side(some[1], 1)

    half = slots // 2
    table = np.stack(
        [spread([0, 1] + arriving(c, first_slots) + arriving(c, last_slots)) for c in range(2)]
    )
    keep_to = np.stack([spread(side(back[c], 0) + [0, 1]) for c in range(2)], axis=1)
    give_to = np.stack([spread(side(back[1 - c], 1)) for c in range(2)], axis=1)
    cut = 2 * rows * half
    rest_to = np.concatenate([give_to[cut:], keep_to])

    own = call(
        functools.partial(own_kernel, devices),
        bf16((rows, features + width)),
        [in_hbm(v) for v in (thinker_rows, expert_ids.T, gate_weights.T, talker_slot)],
        megabytes=4,
    )
    pair = call(pair_kernel, bf16((2 * rows, features + width)), [own, near(own)])
    pair, w_up, w_down = lax.optimization_barrier((pair, w_up, w_down))
    mine = [far(pair, lists, j) for j in range(slots)]
    w_up_here, w_down_here = call(
        fetch_kernel,
        [bf16(w_up.shape[1:]), bf16(w_down.shape[1:])],
        [in_hbm(w_up[0]), in_hbm(w_down[0])],
        in_specs=[pl.BlockSpec(memory_space=pltpu.HBM)] * 2,
        scratch=[pltpu.SemaphoreType.DMA((2,))],
        cost=pl.CostEstimate(flops=0, bytes_accessed=4 * w_up.size, transcendentals=0),
    )
    early_parts = [pair] + [mine[j] for j in first_slots] + [near(mine[j], j) for j in first_slots]
    early_rows = sum(p.shape[0] for p in early_parts)
    early = call(
        functools.partial(early_kernel, devices),
        bf16((early_rows, hidden)),
        [w_gate[0], w_up_here] + early_parts,
        scratch=[pltpu.VMEM((early_rows, features + width), jnp.bfloat16)],
        megabytes=10,
        cost=pl.CostEstimate(
            flops=4 * early_rows * features * hidden,
            bytes_accessed=4 * w_up.size,
            transcendentals=0,
        ),
    )
    late_parts = [mine[j] for j in last_slots]
    late_parts += [near(mine[j], j) for j in last_slots]
    late_rows = sum(p.shape[0] for p in late_parts)
    parts = early_parts + late_parts
    total = early_rows + late_rows
    give, inner = call(
        functools.partial(late_kernel, devices, rows),
        [bf16((cut, features)), bf16((total, hidden))],
        [table, give_to[:cut], w_gate[0], w_up_here, w_down_here, early] + late_parts,
        scratch=[pltpu.VMEM((late_rows, features + width), jnp.bfloat16)],
        megabytes=12,
    )
    given = [near(give)]
    give, *keep, here = call(
        functools.partial(down_kernel, rows),
        [bf16((cut, features))] * 3 + [bf16((2 * rows, features))],
        [table, rest_to, w_down_here, inner],
        megabytes=6,
        cost=pl.CostEstimate(
            flops=2 * rest_to.shape[0] * features * hidden,
            bytes_accessed=2 * w_down.size,
            transcendentals=0,
        ),
    )
    given.append(near(give))
    chip_sum = []
    for k in range(2):
        chip_sum += call(sum_kernel, [bf16((2 * rows, features))] * half, [keep[k], given[k]])
    arrived = [far(chip_sum[j], back, j) for j in range(slots)]
    context, _ = lax.optimization_barrier((left_context.transpose(1, 0, 2), chip_sum[-1]))
    rest, base = call(
        functools.partial(prepare_kernel, len(parts), rows),
        [
            bf16((rows, features)),
            jax.ShapeDtypeStruct((rows, horizon, talker_width), jnp.float32),
        ],
        [table, context, frame_offset, conv_weight] + parts,
        scratch=[pltpu.VMEM((total, features), jnp.bfloat16)],
        megabytes=8,
        cost=pl.CostEstimate(
            flops=2 * rows * total * features, bytes_accessed=2 * total * features, transcendentals=0
        ),
    )
    arrived[0], rest, base = lax.optimization_barrier((arrived[0], rest, base))
    partial = here.astype(jnp.float32)
    for a in arrived:
        partial = partial + a.astype(jnp.float32)
    got = near(partial[rows:].astype(jnp.bfloat16))
    return call(
        owner_kernel,
        bf16((rows, horizon, talker_width)),
        [speech_count, partial, got, rest, talker_proj, base, conv_weight],
        scalars=1,
        megabytes=8,
    )


def local(thinker_rows, *rest):
    devices = lax.axis_size("ep")
    rows = thinker_rows.shape[0]
    small = rows <= CAP and rows == devices and devices >= 8 and devices & (devices - 1) == 0
    if not small:
        return local_dispatch(thinker_rows, *rest)
    return local_gather(thinker_rows, *rest)


def solution(mesh):
    in_specs = (
        P(("groups", "ep"), None),
        P(("groups", "ep"), None),
        P(("groups", "ep"), None),
        P("ep", None, None),
        P("ep", None, None),
        P("ep", None, None),
        P(),
        P(("groups", "ep"), None),
        P(("groups", "ep")),
        P(("groups", "ep"), None, None),
        P(),
        P(),
    )
    out_specs = P(("groups", "ep"), None, None)
    return jax.shard_map(local, mesh=mesh, in_specs=in_specs, out_specs=out_specs, check_vma=False)
```

profile of v0, /device:TPU:0, one launch (start us, length us, event | category | flops | bytes accessed | tf_op | source)
XLA Modules:
  0.0 45.6 jit_solution(6851180916414349739)
XLA Ops:
  0.0 1.0 %shard_map.145.own_ref = bf16[16,2176]{1,0:T(8,128)(2,1)S(1)} custom-call(bf16[16,2048]{1,0:T(8,128)(2,1)} %rows_ref.1, s32[8,16]{1,0:T(8,128)} %bitcast.11, f32[8,16]{1,0:T(8,128)} %bitcast.12, s32[1,16]{1,0:T(1,128)} %slot_ref.1), custom_call_target="tpu_custom_call" | custom-call | tf_op jit(solution)/shard_map/pallas_call | solution.py:306
  1.0 0.6 %collective-permute-start = (bf16[16,2176]{1,0:T(8,128)(2,1)S(1)}, bf16[16,2176]{1,0:T(8,128)(2,1)S(1)}, u32[]{:S(2)}, u32[]{:S(2)}) collective-permute-start(bf16[16,2176]{1,0:T(8,128)(2,1)S(1)} %shard_map.145.own_ref), channel_id=1, source_target_pairs={{0,1},{1,0},{2,3},{3,2},{4,5},{5,4},{6,7},{7,6},{8,9},{9,8},{10,11... | collective-permute-start | bytes 208904 | tf_op jit(solution)/shard_map/ppermute | solution.py:348
  1.6 0.9 %collective-permute-done.other_ref = bf16[16,2176]{1,0:T(8,128)(2,1)S(1)} collective-permute-done((bf16[16,2176]{1,0:T(8,128)(2,1)S(1)}, bf16[16,2176]{1,0:T(8,128)(2,1)S(1)}, u32[]{:S(2)}, u32[]{:S(2)}) %collective-permute-start) | collective-permute-done | bytes 69664 | tf_op jit(solution)/shard_map/ppermute | solution.py:348
  2.5 0.7 %collective-permute-start.2 = (bf16[32,2176]{1,0:T(8,128)(2,1)S(1)}, bf16[32,2176]{1,0:T(8,128)(2,1)S(1)}, u32[]{:S(2)}, u32[]{:S(2)}) collective-permute-start(bf16[32,2176]{1,0:T(8,128)(2,1)S(1)} %shard_map.146.refs_0_), channel_id=1, source_target_pairs={{1,3},{3,1},{5,7},{7,5},{9,11},{11,9},{13,15},{15,13},{17,19},{19,... | collective-permute-start | bytes 417800 | tf_op jit(solution)/shard_map/ppermute | solution.py:344
  3.2 5.0 %collective-permute-start.1 = (bf16[32,2176]{1,0:T(8,128)(2,1)S(1)}, bf16[32,2176]{1,0:T(8,128)(2,1)S(1)}, u32[]{:S(2)}, u32[]{:S(2)}) collective-permute-start(bf16[32,2176]{1,0:T(8,128)(2,1)S(1)} %shard_map.146.refs_0_), channel_id=1, source_target_pairs={{0,12},{1,15},{2,14},{3,13},{4,8},{5,11},{6,10},{7,9},{8,4},{9,7},... | collective-permute-start | bytes 417800 | tf_op jit(solution)/shard_map/ppermute | solution.py:344
  8.2 0.5 %collective-permute-start.6 = (bf16[32,2176]{1,0:T(8,128)(2,1)S(1)}, bf16[32,2176]{1,0:T(8,128)(2,1)S(1)}, u32[]{:S(2)}, u32[]{:S(2)}) collective-permute-start(bf16[32,2176]{1,0:T(8,128)(2,1)S(1)} %shard_map.146.refs_0_), channel_id=1, source_target_pairs={{0,6},{1,11},{2,4},{3,9},{4,2},{5,15},{6,0},{7,13},{8,14},{9,3},{1... | collective-permute-start | bytes 417800 | tf_op jit(solution)/shard_map/ppermute | solution.py:344
  8.7 2.5 %collective-permute-start.5 = (bf16[32,2176]{1,0:T(8,128)(2,1)S(1)}, bf16[32,2176]{1,0:T(8,128)(2,1)S(1)}, u32[]{:S(2)}, u32[]{:S(2)}) collective-permute-start(bf16[32,2176]{1,0:T(8,128)(2,1)S(1)} %shard_map.146.refs_0_), channel_id=1, source_target_pairs={{0,4},{1,9},{2,6},{3,11},{4,0},{5,13},{6,2},{7,15},{8,12},{9,1},{1... | collective-permute-start | bytes 417800 | tf_op jit(solution)/shard_map/ppermute | solution.py:344
  11.2 1.3 %collective-permute-start.4 = (bf16[32,2176]{1,0:T(8,128)(2,1)S(1)}, bf16[32,2176]{1,0:T(8,128)(2,1)S(1)}, u32[]{:S(2)}, u32[]{:S(2)}) collective-permute-start(bf16[32,2176]{1,0:T(8,128)(2,1)S(1)} %collective-permute-done.2.refs_2_), channel_id=1, source_target_pairs={{1,0},{3,2},{5,4},{7,6},{9,8},{11,10},{13,12},{15,14},{17,16},{19,... | collective-permute-start | bytes 417800 | tf_op jit(solution)/shard_map/ppermute | solution.py:348
  12.5 2.8 %collective-permute-start.3 = (bf16[32,2176]{1,0:T(8,128)(2,1)S(1)}, bf16[32,2176]{1,0:T(8,128)(2,1)S(1)}, u32[]{:S(2)}, u32[]{:S(2)}) collective-permute-start(bf16[32,2176]{1,0:T(8,128)(2,1)S(1)} %collective-permute-done.1.refs_1_), channel_id=1, source_target_pairs={{0,1},{1,0},{2,3},{3,2},{4,5},{5,4},{6,7},{7,6},{8,9},{9,8},{10,11... | collective-permute-start | bytes 417800 | tf_op jit(solution)/shard_map/ppermute | solution.py:348
  15.6 4.9 %collective-permute-start.8 = (bf16[32,2176]{1,0:T(8,128)(2,1)S(1)}, bf16[32,2176]{1,0:T(8,128)(2,1)S(1)}, u32[]{:S(2)}, u32[]{:S(2)}) collective-permute-start(bf16[32,2176]{1,0:T(8,128)(2,1)S(1)} %collective-permute-done.6.refs_1_.refs_6_), channel_id=1, source_target_pairs={{0,1},{1,0},{2,3},{3,2},{4,5},{5,4},{6,7},{7,6},{8,9},{9,8},{10,11... | collective-permute-start | bytes 417800 | tf_op jit(solution)/shard_map/ppermute | solution.py:348
  20.9 2.4 %shard_map.147 = (bf16[2048,512]{1,0:T(8,128)(2,1)S(1)}, bf16[512,2048]{1,0:T(8,128)(2,1)S(1)}) custom-call(bf16[2048,512]{1,0:T(8,128)(2,1)} %bitcast.9, bf16[512,2048]{1,0:T(8,128)(2,1)} %bitcast.10), custom_call_target="tpu_custom_call" | custom-call | bytes 4194304 | tf_op jit(solution)/shard_map/pallas_call | solution.py:306
  23.8 0.9 %shard_map.148.early_ref = bf16[160,512]{1,0:T(8,128)(2,1)S(1)} custom-call(bf16[2048,512]{1,0:T(8,128)(2,1)S(1)} %bitcast.6, bf16[2048,512]{1,0:T(8,128)(2,1)S(1)} %get-tuple-element.29.wu_ref, bf16[32,2176]{1,0:T(8,128)(2,1)S(1)} %shard_map.146.refs_0_, bf16[32,2176]{1,0:T(8,128)(2,1)S(1)} %collective-permute-done.1.refs_1_, ...), custom_call_target="tpu_custom_call" | custom-call | flops 671088640 | bytes 4194304 | tf_op jit(solution)/shard_map/pallas_call | solution.py:306
  24.7 1.3 %shard_map.149 = (bf16[64,2048]{1,0:T(8,128)(2,1)S(1)}, bf16[288,512]{1,0:T(8,128)(2,1)S(1)}) custom-call(s32[2,288]{1,0:T(2,128)S(1)} %copy-done.6, s32[64,2]{1,0:T(8,128)S(1)} %copy-done.5, bf16[2048,512]{1,0:T(8,128)(2,1)S(1)} %bitcast.7, bf16[2048,512]{1,0:T(8,128)(2,1)S(1)} %get-tuple-element.29.wu_ref, bf16[512,2048]{1,0:T(8,128)(2,1)S(1)} %get-tuple-element.28.wd_ref, ...), custom_call_target="tpu_custom_call" | custom-call | tf_op jit(solution)/shard_map/pallas_call | solution.py:306
  26.2 1.0 %shard_map.150 = (bf16[64,2048]{1,0:T(8,128)(2,1)S(1)}, bf16[64,2048]{1,0:T(8,128)(2,1)S(1)}, bf16[64,2048]{1,0:T(8,128)(2,1)S(1)}, bf16[32,2048]{1,0:T(8,128)(2,1)S(1)}) custom-call(s32[2,288]{1,0:T(2,128)S(1)} %copy-done.6, s32[224,2]{1,0:T(8,128)S(1)} %copy-done.4, bf16[512,2048]{1,0:T(8,128)(2,1)S(1)} %get-tuple-element.28.wd_ref, ...), custom_call_target="tpu_custom_call" | custom-call | flops 469762048 | bytes 2097152 | tf_op jit(solution)/shard_map/pallas_call | solution.py:306
  27.2 0.5 %collective-permute-start.11 = (bf16[64,2048]{1,0:T(8,128)(2,1)S(1)}, bf16[64,2048]{1,0:T(8,128)(2,1)S(1)}, u32[]{:S(2)}, u32[]{:S(2)}) collective-permute-start(bf16[64,2048]{1,0:T(8,128)(2,1)S(1)} %get-tuple-element.37), channel_id=1, source_target_pairs={{0,1},{1,0},{2,3},{3,2},{4,5},{5,4},{6,7},{7,6},{8,9},{9,8},{10,11... | collective-permute-start | bytes 786440 | tf_op jit(solution)/shard_map/ppermute | solution.py:348
  27.8 3.6 %collective-permute-start.10 = (bf16[32,2048]{1,0:T(8,128)(2,1)S(1)}, bf16[32,2048]{1,0:T(8,128)(2,1)S(1)}, u32[]{:S(2)}, u32[]{:S(2)}) collective-permute-start(bf16[32,2048]{1,0:T(8,128)(2,1)S(1)} %get-tuple-element.35), channel_id=1, source_target_pairs={{0,14},{1,13},{2,12},{3,15},{4,10},{5,9},{6,8},{7,11},{8,6},{9,5},... | collective-permute-start | bytes 393224 | tf_op jit(solution)/shard_map/ppermute | solution.py:344
  31.6 0.7 %collective-permute-start.14 = (bf16[32,2048]{1,0:T(8,128)(2,1)S(1)}, bf16[32,2048]{1,0:T(8,128)(2,1)S(1)}, u32[]{:S(2)}, u32[]{:S(2)}) collective-permute-start(bf16[32,2048]{1,0:T(8,128)(2,1)S(1)} %get-tuple-element.38), channel_id=1, source_target_pairs={{1,3},{3,1},{5,7},{7,5},{9,11},{11,9},{13,15},{15,13},{17,19},{19,... | collective-permute-start | bytes 393224 | tf_op jit(solution)/shard_map/ppermute | solution.py:344
  32.2 1.8 %collective-permute-start.12 = (bf16[32,2048]{1,0:T(8,128)(2,1)S(1)}, bf16[32,2048]{1,0:T(8,128)(2,1)S(1)}, u32[]{:S(2)}, u32[]{:S(2)}) collective-permute-start(bf16[32,2048]{1,0:T(8,128)(2,1)S(1)} %get-tuple-element.43), channel_id=1, source_target_pairs={{0,8},{1,11},{2,10},{3,9},{4,12},{5,15},{6,14},{7,13},{8,0},{9,3},... | collective-permute-start | bytes 393224 | tf_op jit(solution)/shard_map/ppermute | solution.py:344
  34.0 0.5 %shard_map.153 = (bf16[16,2048]{1,0:T(8,128)(2,1)S(1)}, f32[16,4,1024]{2,1,0:T(4,128)S(1)}) custom-call(s32[2,288]{1,0:T(2,128)S(1)} %copy-done.6, bf16[6,16,1024]{2,1,0:T(8,128)(2,1)S(1)} %bitcast.8, f32[4,1024]{1,0:T(4,128)S(1)} %copy-done.7, f32[7,1024]{1,0:T(8,128)S(1)} %copy-done.3, bf16[32,2176]{1,0:T(8,128)(2,1)S(1)} %shard_map.146.refs_0_, ...), custom_call_target="tpu_custom_call" | custom-call | flops 18874368 | bytes 1179648 | tf_op jit(solution)/shard_map/pallas_call | solution.py:306
  34.5 2.5 %collective-permute-done.10 = bf16[32,2048]{1,0:T(8,128)(2,1)S(1)} collective-permute-done((bf16[32,2048]{1,0:T(8,128)(2,1)S(1)}, bf16[32,2048]{1,0:T(8,128)(2,1)S(1)}, u32[]{:S(2)}, u32[]{:S(2)}) %collective-permute-start.10) | collective-permute-done | bytes 131104 | tf_op jit(solution)/shard_map/ppermute | solution.py:344
  37.0 4.5 %collective-permute-done.13 = bf16[32,2048]{1,0:T(8,128)(2,1)S(1)} collective-permute-done((bf16[32,2048]{1,0:T(8,128)(2,1)S(1)}, bf16[32,2048]{1,0:T(8,128)(2,1)S(1)}, u32[]{:S(2)}, u32[]{:S(2)}) %collective-permute-start.13) | collective-permute-done | bytes 131104 | tf_op jit(solution)/shard_map/ppermute | solution.py:344
  41.5 0.6 %collective-permute-done.12 = bf16[32,2048]{1,0:T(8,128)(2,1)S(1)} collective-permute-done((bf16[32,2048]{1,0:T(8,128)(2,1)S(1)}, bf16[32,2048]{1,0:T(8,128)(2,1)S(1)}, u32[]{:S(2)}, u32[]{:S(2)}) %collective-permute-start.12) | collective-permute-done | bytes 131104 | tf_op jit(solution)/shard_map/ppermute | solution.py:344
  42.5 1.1 %collective-permute-done.15.got_ref = bf16[16,2048]{1,0:T(8,128)(2,1)S(1)} collective-permute-done((bf16[16,2048]{1,0:T(8,128)(2,1)S(1)}, bf16[16,2048]{1,0:T(8,128)(2,1)S(1)}, u32[]{:S(2)}, u32[]{:S(2)}) %collective-permute-start.15) | collective-permute-done | bytes 65568 | tf_op jit(solution)/shard_map/ppermute | solution.py:348
  43.5 2.1 %shard_map.154 = bf16[16,4,1024]{2,1,0:T(4,128)(2,1)} custom-call(s32[16]{0:T(128)S(1)} %copy-done.8, f32[32,2048]{1,0:T(8,128)S(1)} %convert_add_fusion.mine_ref, bf16[16,2048]{1,0:T(8,128)(2,1)S(1)} %collective-permute-done.15.got_ref, bf16[16,2048]{1,0:T(8,128)(2,1)S(1)} %get-tuple-element.45.rest_ref, bf16[2048,1024]{1,0:T(8,128)(2,1)S(1)} %copy-done.1, ...), custom_call_target="tpu_custom_call" | custom-call | tf_op jit(solution)/shard_map/pallas_call | solution.py:306
  (38 shorter events, 1.9 us)
Async XLA Ops:
  1.0 1.5 %collective-permute-start = (bf16[16,2176]{1,0:T(8,128)(2,1)S(1)}, bf16[16,2176]{1,0:T(8,128)(2,1)S(1)}, u32[]{:S(2)}, u32[]{:S(2)}) collective-permute-start(bf16[16,2176]{1,0:T(8,128)(2,1)S(1)} %shard_map.145.own_ref), channel_id=1, source_target_pairs={{0,1},{1,0},{2,3},{3,2},{4,5},{5,4},{6,7},{7,6},{8,9},{9,8},{10,11... | collective-permute-start | bytes 208904 | tf_op jit(solution)/shard_map/ppermute | solution.py:348
  2.5 8.7 %collective-permute-start.2 = (bf16[32,2176]{1,0:T(8,128)(2,1)S(1)}, bf16[32,2176]{1,0:T(8,128)(2,1)S(1)}, u32[]{:S(2)}, u32[]{:S(2)}) collective-permute-start(bf16[32,2176]{1,0:T(8,128)(2,1)S(1)} %shard_map.146.refs_0_), channel_id=1, source_target_pairs={{1,3},{3,1},{5,7},{7,5},{9,11},{11,9},{13,15},{15,13},{17,19},{19,... | collective-permute-start | bytes 417800 | tf_op jit(solution)/shard_map/ppermute | solution.py:344
  3.2 9.3 %collective-permute-start.1 = (bf16[32,2176]{1,0:T(8,128)(2,1)S(1)}, bf16[32,2176]{1,0:T(8,128)(2,1)S(1)}, u32[]{:S(2)}, u32[]{:S(2)}) collective-permute-start(bf16[32,2176]{1,0:T(8,128)(2,1)S(1)} %shard_map.146.refs_0_), channel_id=1, source_target_pairs={{0,12},{1,15},{2,14},{3,13},{4,8},{5,11},{6,10},{7,9},{8,4},{9,7},... | collective-permute-start | bytes 417800 | tf_op jit(solution)/shard_map/ppermute | solution.py:344
  8.2 7.4 %collective-permute-start.6 = (bf16[32,2176]{1,0:T(8,128)(2,1)S(1)}, bf16[32,2176]{1,0:T(8,128)(2,1)S(1)}, u32[]{:S(2)}, u32[]{:S(2)}) collective-permute-start(bf16[32,2176]{1,0:T(8,128)(2,1)S(1)} %shard_map.146.refs_0_), channel_id=1, source_target_pairs={{0,6},{1,11},{2,4},{3,9},{4,2},{5,15},{6,0},{7,13},{8,14},{9,3},{1... | collective-permute-start | bytes 417800 | tf_op jit(solution)/shard_map/ppermute | solution.py:344
  8.7 11.8 %collective-permute-start.5 = (bf16[32,2176]{1,0:T(8,128)(2,1)S(1)}, bf16[32,2176]{1,0:T(8,128)(2,1)S(1)}, u32[]{:S(2)}, u32[]{:S(2)}) collective-permute-start(bf16[32,2176]{1,0:T(8,128)(2,1)S(1)} %shard_map.146.refs_0_), channel_id=1, source_target_pairs={{0,4},{1,9},{2,6},{3,11},{4,0},{5,13},{6,2},{7,15},{8,12},{9,1},{1... | collective-permute-start | bytes 417800 | tf_op jit(solution)/shard_map/ppermute | solution.py:344
  11.2 12.1 %collective-permute-start.4 = (bf16[32,2176]{1,0:T(8,128)(2,1)S(1)}, bf16[32,2176]{1,0:T(8,128)(2,1)S(1)}, u32[]{:S(2)}, u32[]{:S(2)}) collective-permute-start(bf16[32,2176]{1,0:T(8,128)(2,1)S(1)} %collective-permute-done.2.refs_2_), channel_id=1, source_target_pairs={{1,0},{3,2},{5,4},{7,6},{9,8},{11,10},{13,12},{15,14},{17,16},{19,... | collective-permute-start | bytes 417800 | tf_op jit(solution)/shard_map/ppermute | solution.py:348
  12.5 10.9 %collective-permute-start.3 = (bf16[32,2176]{1,0:T(8,128)(2,1)S(1)}, bf16[32,2176]{1,0:T(8,128)(2,1)S(1)}, u32[]{:S(2)}, u32[]{:S(2)}) collective-permute-start(bf16[32,2176]{1,0:T(8,128)(2,1)S(1)} %collective-permute-done.1.refs_1_), channel_id=1, source_target_pairs={{0,1},{1,0},{2,3},{3,2},{4,5},{5,4},{6,7},{7,6},{8,9},{9,8},{10,11... | collective-permute-start | bytes 417800 | tf_op jit(solution)/shard_map/ppermute | solution.py:348
  15.6 9.1 %collective-permute-start.8 = (bf16[32,2176]{1,0:T(8,128)(2,1)S(1)}, bf16[32,2176]{1,0:T(8,128)(2,1)S(1)}, u32[]{:S(2)}, u32[]{:S(2)}) collective-permute-start(bf16[32,2176]{1,0:T(8,128)(2,1)S(1)} %collective-permute-done.6.refs_1_.refs_6_), channel_id=1, source_target_pairs={{0,1},{1,0},{2,3},{3,2},{4,5},{5,4},{6,7},{7,6},{8,9},{9,8},{10,11... | collective-permute-start | bytes 417800 | tf_op jit(solution)/shard_map/ppermute | solution.py:348
  20.5 4.2 %collective-permute-start.7 = (bf16[32,2176]{1,0:T(8,128)(2,1)S(1)}, bf16[32,2176]{1,0:T(8,128)(2,1)S(1)}, u32[]{:S(2)}, u32[]{:S(2)}) collective-permute-start(bf16[32,2176]{1,0:T(8,128)(2,1)S(1)} %collective-permute-done.5.refs_0_.refs_5_), channel_id=1, source_target_pairs={{0,1},{1,0},{2,3},{3,2},{4,5},{5,4},{6,7},{7,6},{8,9},{9,8},{10,11... | collective-permute-start | bytes 417800 | tf_op jit(solution)/shard_map/ppermute | solution.py:348
  20.9 2.9 %copy-start = (bf16[1,2048,512]{2,1,0:T(8,128)(2,1)S(1)}, bf16[1,2048,512]{2,1,0:T(8,128)(2,1)}, u32[]{:S(2)}) copy-start(bf16[1,2048,512]{2,1,0:T(8,128)(2,1)} %param.18) | copy-start | bytes 6291460
  23.8 0.9 %copy-start.6 = (s32[2,288]{1,0:T(2,128)S(1)}, s32[2,288]{1,0:T(2,128)}, u32[]{:S(2)}) copy-start(s32[2,288]{1,0:T(2,128)} %constant.6.clone.table_ref) | copy-start | bytes 6916
  24.7 1.5 %copy-start.4 = (s32[224,2]{1,0:T(8,128)S(1)}, s32[224,2]{1,0:T(8,128)}, u32[]{:S(2)}) copy-start(s32[224,2]{1,0:T(8,128)} %constant.8.clone.target_ref) | copy-start | bytes 5380
  26.0 8.0 %copy-start.2 = (bf16[16,6,1024]{2,0,1:T(8,128)(2,1)S(1)}, bf16[16,6,1024]{2,0,1:T(8,128)(2,1)}, u32[]{:S(2)}) copy-start(bf16[16,6,1024]{2,0,1:T(8,128)(2,1)} %param.24) | copy-start | bytes 589828
  26.0 8.0 %copy-start.3 = (f32[7,1024]{1,0:T(8,128)S(1)}, f32[7,1024]{1,0:T(8,128)}, u32[]{:S(2)}) copy-start(f32[7,1024]{1,0:T(8,128)} %conv_ref.3) | copy-start | bytes 86020
  26.1 8.0 %copy-start.7 = (f32[4,1024]{1,0:T(4,128)S(1)}, f32[4,1024]{1,0:T(4,128)}, u32[]{:S(2)}) copy-start(f32[4,1024]{1,0:T(4,128)} %offset_ref.1) | copy-start | bytes 49156
  26.1 1.7 %collective-permute-start.9 = (bf16[64,2048]{1,0:T(8,128)(2,1)S(1)}, bf16[64,2048]{1,0:T(8,128)(2,1)S(1)}, u32[]{:S(2)}, u32[]{:S(2)}) collective-permute-start(bf16[64,2048]{1,0:T(8,128)(2,1)S(1)} %get-tuple-element.34), channel_id=1, source_target_pairs={{0,1},{1,0},{2,3},{3,2},{4,5},{5,4},{6,7},{7,6},{8,9},{9,8},{10,11... | collective-permute-start | bytes 786440 | tf_op jit(solution)/shard_map/ppermute | solution.py:348
  26.2 17.3 %copy-start.1 = (bf16[2048,1024]{1,0:T(8,128)(2,1)S(1)}, bf16[2048,1024]{1,0:T(8,128)(2,1)}, u32[]{:S(2)}) copy-start(bf16[2048,1024]{1,0:T(8,128)(2,1)} %proj_ref.1) | copy-start | bytes 12582916
  27.2 16.3 %copy-start.8 = (s32[16]{0:T(128)S(1)}, s32[16]{0:T(128)}, u32[]{:S(2)}) copy-start(s32[16]{0:T(128)} %count_ref.1) | copy-start | bytes 196
  27.2 4.2 %collective-permute-start.11 = (bf16[64,2048]{1,0:T(8,128)(2,1)S(1)}, bf16[64,2048]{1,0:T(8,128)(2,1)S(1)}, u32[]{:S(2)}, u32[]{:S(2)}) collective-permute-start(bf16[64,2048]{1,0:T(8,128)(2,1)S(1)} %get-tuple-element.37), channel_id=1, source_target_pairs={{0,1},{1,0},{2,3},{3,2},{4,5},{5,4},{6,7},{7,6},{8,9},{9,8},{10,11... | collective-permute-start | bytes 786440 | tf_op jit(solution)/shard_map/ppermute | solution.py:348
  27.8 9.2 %collective-permute-start.10 = (bf16[32,2048]{1,0:T(8,128)(2,1)S(1)}, bf16[32,2048]{1,0:T(8,128)(2,1)S(1)}, u32[]{:S(2)}, u32[]{:S(2)}) collective-permute-start(bf16[32,2048]{1,0:T(8,128)(2,1)S(1)} %get-tuple-element.35), channel_id=1, source_target_pairs={{0,14},{1,13},{2,12},{3,15},{4,10},{5,9},{6,8},{7,11},{8,6},{9,5},... | collective-permute-start | bytes 393224 | tf_op jit(solution)/shard_map/ppermute | solution.py:344
  31.5 10.0 %collective-permute-start.13 = (bf16[32,2048]{1,0:T(8,128)(2,1)S(1)}, bf16[32,2048]{1,0:T(8,128)(2,1)S(1)}, u32[]{:S(2)}, u32[]{:S(2)}) collective-permute-start(bf16[32,2048]{1,0:T(8,128)(2,1)S(1)} %get-tuple-element.44), channel_id=1, source_target_pairs={{0,6},{1,5},{2,4},{3,7},{4,2},{5,1},{6,0},{7,3},{8,14},{9,13},{10,... | collective-permute-start | bytes 393224 | tf_op jit(solution)/shard_map/ppermute | solution.py:344
  31.6 9.9 %collective-permute-start.14 = (bf16[32,2048]{1,0:T(8,128)(2,1)S(1)}, bf16[32,2048]{1,0:T(8,128)(2,1)S(1)}, u32[]{:S(2)}, u32[]{:S(2)}) collective-permute-start(bf16[32,2048]{1,0:T(8,128)(2,1)S(1)} %get-tuple-element.38), channel_id=1, source_target_pairs={{1,3},{3,1},{5,7},{7,5},{9,11},{11,9},{13,15},{15,13},{17,19},{19,... | collective-permute-start | bytes 393224 | tf_op jit(solution)/shard_map/ppermute | solution.py:344
  32.2 9.9 %collective-permute-start.12 = (bf16[32,2048]{1,0:T(8,128)(2,1)S(1)}, bf16[32,2048]{1,0:T(8,128)(2,1)S(1)}, u32[]{:S(2)}, u32[]{:S(2)}) collective-permute-start(bf16[32,2048]{1,0:T(8,128)(2,1)S(1)} %get-tuple-element.43), channel_id=1, source_target_pairs={{0,8},{1,11},{2,10},{3,9},{4,12},{5,15},{6,14},{7,13},{8,0},{9,3},... | collective-permute-start | bytes 393224 | tf_op jit(solution)/shard_map/ppermute | solution.py:344
  42.2 1.3 %collective-permute-start.15 = (bf16[16,2048]{1,0:T(8,128)(2,1)S(1)}, bf16[16,2048]{1,0:T(8,128)(2,1)S(1)}, u32[]{:S(2)}, u32[]{:S(2)}) collective-permute-start(bf16[16,2048]{1,0:T(8,128)(2,1)S(1)} %slice.7), channel_id=1, source_target_pairs={{0,1},{1,0},{2,3},{3,2},{4,5},{5,4},{6,7},{7,6},{8,9},{9,8},{10,11... | collective-permute-start | bytes 196616 | tf_op jit(solution)/shard_map/ppermute | solution.py:348
  (1 other events, 0.9 us)
where the time goes:
time: 45.8 us; the launch traced here: 45.6 us
  starting transfers between devices  25.7 us (56%)
  waiting for transfers between devices  9.84 us (21%)
  Pallas kernels  9.32 us (20%)
  local copies, waits for them, and re-layouts  0.49 us (1%)
    ppermute x8, starting transfers between devices, far(): return lax.ppermute(x, 'ep', pairs)  14.8 us
    ppermute x8, starting transfers between devices, near(): return lax.ppermute(x, 'ep', pairs)  10.9 us
    pallas_call x10, Pallas kernels, call(): pl.pallas_call(kernel, out_shape=out_shape, in_specs=in_specs or specs, o...  9.32 us
    ppermute x8, waiting for transfers between devices, far(): return lax.ppermute(x, 'ep', pairs)  7.85 us
    ppermute x8, waiting for transfers between devices, near(): return lax.ppermute(x, 'ep', pairs)  1.99 us
  transfers between devices with their start and end apart: 16, of which 6 were waited for; matrix products, arithmetic and copies ran while one was open for 0% of the time, Pallas kernels for 11%

commit v1 on v0

--- a/solution.py
+++ b/solution.py
@@ -194,17 +194,18 @@
 
 
 def late_kernel(experts, rows, table_ref, target_ref, wg_ref, wu_ref, wd_ref, early_ref, *refs):
-    parts, (out_ref, inner_ref, x_ref) = refs[:-3], refs[-3:]
+    parts, (out_ref, placed_ref, inner_ref, x_ref) = refs[:-4], refs[-4:]
     first = early_ref.shape[0]
     inner_ref[:first, :] = early_ref[...]
     activate(experts, parts, wg_ref, wu_ref, x_ref, inner_ref, first)
-    down_kernel(rows, table_ref, target_ref, wd_ref, inner_ref, out_ref)
-
-
-def down_kernel(rows, table_ref, target_ref, wd_ref, inner_ref, *outs):
-    me = lax.axis_index("ep")
-    move = move_rows(me, rows, table_ref, target_ref)
+    move = move_rows(lax.axis_index("ep"), rows, table_ref, target_ref)
     placed = dot32(move, inner_ref[...]).astype(jnp.bfloat16)
+    cut = out_ref.shape[0]
+    placed_ref[...] = placed[cut:]
+    down(placed[:cut], wd_ref, [out_ref])
+
+
+def down(placed, wd_ref, outs):
     features = wd_ref.shape[1]
     step = min(512, features)
     for n in range(0, features, step):
@@ -215,6 +216,10 @@
             at += out.shape[0]
 
 
+def rest_kernel(placed_ref, wd_ref, *outs):
+    down(placed_ref[...], wd_ref, outs)
+
+
 def sum_kernel(ours_ref, given_ref, *outs):
     at = 0
     for out in outs:
@@ -224,8 +229,10 @@
         at += out.shape[0]
 
 
-def prepare_kernel(blocks, rows, table_ref, context_ref, offset_ref, conv_ref, *refs):
-    parts, (rest_ref, base_ref, x_ref) = refs[:blocks], refs[blocks:]
+def prepare_kernel(
+    blocks, rows, count_ref, table_ref, context_ref, offset_ref, conv_ref, *refs
+):
+    parts, (rest_ref, base_ref, scale_ref, x_ref) = refs[:blocks], refs[blocks:]
     me = lax.axis_index("ep")
     features = rest_ref.shape[1]
     at = 0
@@ -240,20 +247,25 @@
     rest_ref[...] = dot32(pick, x_ref[...]).astype(jnp.bfloat16)
     taps, horizon, past = conv_ref.shape[0], offset_ref.shape[0], context_ref.shape[0]
     context = [context_ref[i].astype(jnp.float32) for i in range(past)]
+    stream = lax.broadcasted_iota(jnp.int32, (rows, 1), 0)
+    count = jnp.zeros((rows, 1), jnp.int32)
+    for q in range(rows):
+        count = jnp.where(stream == q, count_ref[q], count)
     for f in range(horizon):
         fixed = jnp.zeros((1, conv_ref.shape[1]), jnp.float32)
+        scale = jnp.zeros((1, conv_ref.shape[1]), jnp.float32)
         for t in range(past - f, taps):
             i = f + t - past
             fixed = fixed + conv_ref[t : t + 1, :] * offset_ref[i : i + 1, :]
+            scale = scale + conv_ref[t : t + 1, :]
         total = jnp.broadcast_to(fixed, context[0].shape)
         for t in range(past - f):
             total = total + conv_ref[t : t + 1, :] * context[f + t]
-        base_ref[:, f, :] = total
-
-
-def owner_kernel(
-    count_ref, mine_ref, got_ref, rest_ref, proj_ref, base_ref, conv_ref, out_ref
-):
+        base_ref[:, f, :] = jnp.where(f < count, total, 0.0)
+        scale_ref[:, f, :] = jnp.where(f < count, jnp.broadcast_to(scale, total.shape), 0.0)
+
+
+def owner_kernel(mine_ref, got_ref, rest_ref, proj_ref, base_ref, scale_ref, out_ref):
     me = lax.axis_index("ep")
     rows = rest_ref.shape[0]
     total = mine_ref[:rows, :] + got_ref[...].astype(jnp.float32)
@@ -265,14 +277,9 @@
     two = lax.broadcasted_iota(jnp.int32, (rows, rows), 1)
     order = jnp.where((one ^ two) == me, 1.0, 0.0).astype(jnp.bfloat16)
     owned = dot32(order, talker)
-    taps, horizon = conv_ref.shape[0], base_ref.shape[1]
-    frame = lax.broadcasted_iota(jnp.int32, (horizon, owned.shape[1]), 0)
-    scale = jnp.zeros(frame.shape, jnp.float32)
-    for t in range(taps):
-        scale = scale + jnp.where(frame + t >= taps - 1, conv_ref[t : t + 1, :], 0.0)
     for q in range(rows):
-        voice = base_ref[q] + scale * owned[q : q + 1, :]
-        out_ref[q] = jnp.where(frame < count_ref[q], voice, 0.0).astype(jnp.bfloat16)
+        voice = base_ref[q] + scale_ref[q] * owned[q : q + 1, :]
+        out_ref[q] = voice.astype(jnp.bfloat16)
 
 
 def vmem(count):
@@ -367,7 +374,7 @@
     keep_to = np.stack([spread(side(back[c], 0) + [0, 1]) for c in range(2)], axis=1)
     give_to = np.stack([spread(side(back[1 - c], 1)) for c in range(2)], axis=1)
     cut = 2 * rows * half
-    rest_to = np.concatenate([give_to[cut:], keep_to])
+    target = np.concatenate([give_to, keep_to])
 
     own = call(
         functools.partial(own_kernel, devices),
@@ -405,21 +412,24 @@
     late_rows = sum(p.shape[0] for p in late_parts)
     parts = early_parts + late_parts
     total = early_rows + late_rows
-    give, inner = call(
+    give, placed = call(
         functools.partial(late_kernel, devices, rows),
-        [bf16((cut, features)), bf16((total, hidden))],
-        [table, give_to[:cut], w_gate[0], w_up_here, w_down_here, early] + late_parts,
-        scratch=[pltpu.VMEM((late_rows, features + width), jnp.bfloat16)],
+        [bf16((cut, features)), bf16((target.shape[0] - cut, hidden))],
+        [table, target, w_gate[0], w_up_here, w_down_here, early] + late_parts,
+        scratch=[
+            pltpu.VMEM((total, hidden), jnp.bfloat16),
+            pltpu.VMEM((late_rows, features + width), jnp.bfloat16),
+        ],
         megabytes=12,
     )
     given = [near(give)]
     give, *keep, here = call(
-        functools.partial(down_kernel, rows),
+        rest_kernel,
         [bf16((cut, features))] * 3 + [bf16((2 * rows, features))],
-        [table, rest_to, w_down_here, inner],
+        [placed, w_down_here],
         megabytes=6,
         cost=pl.CostEstimate(
-            flops=2 * rest_to.shape[0] * features * hidden,
+            flops=2 * target.shape[0] * features * hidden,
             bytes_accessed=2 * w_down.size,
             transcendentals=0,
         ),
@@ -430,20 +440,19 @@
         chip_sum += call(sum_kernel, [bf16((2 * rows, features))] * half, [keep[k], given[k]])
     arrived = [far(chip_sum[j], back, j) for j in range(slots)]
     context, _ = lax.optimization_barrier((left_context.transpose(1, 0, 2), chip_sum[-1]))
-    rest, base = call(
+    frames = jax.ShapeDtypeStruct((rows, horizon, talker_width), jnp.float32)
+    rest, base, scale = call(
         functools.partial(prepare_kernel, len(parts), rows),
-        [
-            bf16((rows, features)),
-            jax.ShapeDtypeStruct((rows, horizon, talker_width), jnp.float32),
-        ],
-        [table, context, frame_offset, conv_weight] + parts,
+        [bf16((rows, features)), frames, frames],
+        [speech_count, table, context, frame_offset, conv_weight] + parts,
+        scalars=1,
         scratch=[pltpu.VMEM((total, features), jnp.bfloat16)],
         megabytes=8,
         cost=pl.CostEstimate(
             flops=2 * rows * total * features, bytes_accessed=2 * total * features, transcendentals=0
         ),
     )
-    arrived[0], rest, base = lax.optimization_barrier((arrived[0], rest, base))
+    arrived[0], rest, base, scale = lax.optimization_barrier((arrived[0], rest, base, scale))
     partial = here.astype(jnp.float32)
     for a in arrived:
         partial = partial + a.astype(jnp.float32)
@@ -451,8 +460,7 @@
     return call(
         owner_kernel,
         bf16((rows, horizon, talker_width)),
-        [speech_count, partial, got, rest, talker_proj, base, conv_weight],
-        scalars=1,
+        [partial, got, rest, talker_proj, base, scale],
         megabytes=8,
     )
 

time: 45.8 us -> 45.2 us (0.987)
  waiting for transfers between devices: 9.84 us -> 9.37 us
    ppermute x8, waiting for transfers between devices: 7.85 us -> 7.16 us  [far(): return lax.ppermute(x, 'ep', pairs)]
  transfers between devices with their start and end apart: 16 -> 16, of which waited for: 6 -> 7; matrix products, arithmetic and copies ran while one was open for 0% -> 0% of each run, Pallas kernels for 11% -> 11%
where the time goes in v1:
time: 45.2 us; the launch traced here: 45 us
  starting transfers between devices  25.8 us (57%)
  waiting for transfers between devices  9.37 us (21%)
  Pallas kernels  9.1 us (20%)
  local copies, waits for them, and re-layouts  0.48 us (1%)
    ppermute x8, starting transfers between devices, far(): return lax.ppermute(x, 'ep', pairs)  14.8 us
    ppermute x8, starting transfers between devices, near(): return lax.ppermute(x, 'ep', pairs)  11 us
    pallas_call x10, Pallas kernels, call(): pl.pallas_call(kernel, out_shape=out_shape, in_specs=in_specs or specs, o...  9.1 us
    ppermute x8, waiting for transfers between devices, far(): return lax.ppermute(x, 'ep', pairs)  7.16 us
    ppermute x8, waiting for transfers between devices, near(): return lax.ppermute(x, 'ep', pairs)  2.21 us
  transfers between devices with their start and end apart: 16, of which 7 were waited for; matrix products, arithmetic and copies ran while one was open for 0% of the time, Pallas kernels for 11%

profile of v1, /device:TPU:0, one launch (start us, length us, event | category | flops | bytes accessed | tf_op | source)
XLA Modules:
  0.0 45.0 jit_solution(6488051241586980255)
XLA Ops:
  0.0 1.0 %shard_map.136.own_ref = bf16[16,2176]{1,0:T(8,128)(2,1)S(1)} custom-call(bf16[16,2048]{1,0:T(8,128)(2,1)} %rows_ref.1, s32[8,16]{1,0:T(8,128)} %bitcast.11, f32[8,16]{1,0:T(8,128)} %bitcast.12, s32[1,16]{1,0:T(1,128)} %slot_ref.1), custom_call_target="tpu_custom_call" | custom-call | tf_op jit(solution)/shard_map/pallas_call | solution.py:313
  1.0 0.6 %collective-permute-start = (bf16[16,2176]{1,0:T(8,128)(2,1)S(1)}, bf16[16,2176]{1,0:T(8,128)(2,1)S(1)}, u32[]{:S(2)}, u32[]{:S(2)}) collective-permute-start(bf16[16,2176]{1,0:T(8,128)(2,1)S(1)} %shard_map.136.own_ref), channel_id=1, source_target_pairs={{0,1},{1,0},{2,3},{3,2},{4,5},{5,4},{6,7},{7,6},{8,9},{9,8},{10,11... | collective-permute-start | bytes 208904 | tf_op jit(solution)/shard_map/ppermute | solution.py:355
  1.6 0.9 %collective-permute-done.other_ref = bf16[16,2176]{1,0:T(8,128)(2,1)S(1)} collective-permute-done((bf16[16,2176]{1,0:T(8,128)(2,1)S(1)}, bf16[16,2176]{1,0:T(8,128)(2,1)S(1)}, u32[]{:S(2)}, u32[]{:S(2)}) %collective-permute-start) | collective-permute-done | bytes 69664 | tf_op jit(solution)/shard_map/ppermute | solution.py:355
  2.5 0.7 %collective-permute-start.2 = (bf16[32,2176]{1,0:T(8,128)(2,1)S(1)}, bf16[32,2176]{1,0:T(8,128)(2,1)S(1)}, u32[]{:S(2)}, u32[]{:S(2)}) collective-permute-start(bf16[32,2176]{1,0:T(8,128)(2,1)S(1)} %shard_map.137.refs_0_), channel_id=1, source_target_pairs={{1,3},{3,1},{5,7},{7,5},{9,11},{11,9},{13,15},{15,13},{17,19},{19,... | collective-permute-start | bytes 417800 | tf_op jit(solution)/shard_map/ppermute | solution.py:351
  3.2 5.0 %collective-permute-start.1 = (bf16[32,2176]{1,0:T(8,128)(2,1)S(1)}, bf16[32,2176]{1,0:T(8,128)(2,1)S(1)}, u32[]{:S(2)}, u32[]{:S(2)}) collective-permute-start(bf16[32,2176]{1,0:T(8,128)(2,1)S(1)} %shard_map.137.refs_0_), channel_id=1, source_target_pairs={{0,12},{1,15},{2,14},{3,13},{4,8},{5,11},{6,10},{7,9},{8,4},{9,7},... | collective-permute-start | bytes 417800 | tf_op jit(solution)/shard_map/ppermute | solution.py:351
  8.2 0.5 %collective-permute-start.6 = (bf16[32,2176]{1,0:T(8,128)(2,1)S(1)}, bf16[32,2176]{1,0:T(8,128)(2,1)S(1)}, u32[]{:S(2)}, u32[]{:S(2)}) collective-permute-start(bf16[32,2176]{1,0:T(8,128)(2,1)S(1)} %shard_map.137.refs_0_), channel_id=1, source_target_pairs={{0,6},{1,11},{2,4},{3,9},{4,2},{5,15},{6,0},{7,13},{8,14},{9,3},{1... | collective-permute-start | bytes 417800 | tf_op jit(solution)/shard_map/ppermute | solution.py:351
  8.7 2.5 %collective-permute-start.5 = (bf16[32,2176]{1,0:T(8,128)(2,1)S(1)}, bf16[32,2176]{1,0:T(8,128)(2,1)S(1)}, u32[]{:S(2)}, u32[]{:S(2)}) collective-permute-start(bf16[32,2176]{1,0:T(8,128)(2,1)S(1)} %shard_map.137.refs_0_), channel_id=1, source_target_pairs={{0,4},{1,9},{2,6},{3,11},{4,0},{5,13},{6,2},{7,15},{8,12},{9,1},{1... | collective-permute-start | bytes 417800 | tf_op jit(solution)/shard_map/ppermute | solution.py:351
  11.2 1.3 %collective-permute-start.4 = (bf16[32,2176]{1,0:T(8,128)(2,1)S(1)}, bf16[32,2176]{1,0:T(8,128)(2,1)S(1)}, u32[]{:S(2)}, u32[]{:S(2)}) collective-permute-start(bf16[32,2176]{1,0:T(8,128)(2,1)S(1)} %collective-permute-done.2.refs_2_), channel_id=1, source_target_pairs={{1,0},{3,2},{5,4},{7,6},{9,8},{11,10},{13,12},{15,14},{17,16},{19,... | collective-permute-start | bytes 417800 | tf_op jit(solution)/shard_map/ppermute | solution.py:355
  12.5 2.8 %collective-permute-start.3 = (bf16[32,2176]{1,0:T(8,128)(2,1)S(1)}, bf16[32,2176]{1,0:T(8,128)(2,1)S(1)}, u32[]{:S(2)}, u32[]{:S(2)}) collective-permute-start(bf16[32,2176]{1,0:T(8,128)(2,1)S(1)} %collective-permute-done.1.refs_1_), channel_id=1, source_target_pairs={{0,1},{1,0},{2,3},{3,2},{4,5},{5,4},{6,7},{7,6},{8,9},{9,8},{10,11... | collective-permute-start | bytes 417800 | tf_op jit(solution)/shard_map/ppermute | solution.py:355
  15.6 4.9 %collective-permute-start.8 = (bf16[32,2176]{1,0:T(8,128)(2,1)S(1)}, bf16[32,2176]{1,0:T(8,128)(2,1)S(1)}, u32[]{:S(2)}, u32[]{:S(2)}) collective-permute-start(bf16[32,2176]{1,0:T(8,128)(2,1)S(1)} %collective-permute-done.6.refs_1_.refs_6_), channel_id=1, source_target_pairs={{0,1},{1,0},{2,3},{3,2},{4,5},{5,4},{6,7},{7,6},{8,9},{9,8},{10,11... | collective-permute-start | bytes 417800 | tf_op jit(solution)/shard_map/ppermute | solution.py:355
  20.9 2.4 %shard_map.138 = (bf16[2048,512]{1,0:T(8,128)(2,1)S(1)}, bf16[512,2048]{1,0:T(8,128)(2,1)S(1)}) custom-call(bf16[2048,512]{1,0:T(8,128)(2,1)} %bitcast.9, bf16[512,2048]{1,0:T(8,128)(2,1)} %bitcast.10), custom_call_target="tpu_custom_call" | custom-call | bytes 4194304 | tf_op jit(solution)/shard_map/pallas_call | solution.py:313
  23.8 0.9 %shard_map.139.early_ref = bf16[160,512]{1,0:T(8,128)(2,1)S(1)} custom-call(bf16[2048,512]{1,0:T(8,128)(2,1)S(1)} %bitcast.6, bf16[2048,512]{1,0:T(8,128)(2,1)S(1)} %get-tuple-element.30.wu_ref, bf16[32,2176]{1,0:T(8,128)(2,1)S(1)} %shard_map.137.refs_0_, bf16[32,2176]{1,0:T(8,128)(2,1)S(1)} %collective-permute-done.1.refs_1_, ...), custom_call_target="tpu_custom_call" | custom-call | flops 671088640 | bytes 4194304 | tf_op jit(solution)/shard_map/pallas_call | solution.py:313
  24.7 1.4 %shard_map.140 = (bf16[64,2048]{1,0:T(8,128)(2,1)S(1)}, bf16[224,512]{1,0:T(8,128)(2,1)S(1)}) custom-call(s32[2,288]{1,0:T(2,128)S(1)} %copy-done.6, s32[288,2]{1,0:T(8,128)S(1)} %copy-done.3, bf16[2048,512]{1,0:T(8,128)(2,1)S(1)} %bitcast.7, bf16[2048,512]{1,0:T(8,128)(2,1)S(1)} %get-tuple-element.30.wu_ref, ...), custom_call_target="tpu_custom_call" | custom-call | tf_op jit(solution)/shard_map/pallas_call | solution.py:313
  26.3 0.7 %shard_map.141 = (bf16[64,2048]{1,0:T(8,128)(2,1)S(1)}, bf16[64,2048]{1,0:T(8,128)(2,1)S(1)}, bf16[64,2048]{1,0:T(8,128)(2,1)S(1)}, bf16[32,2048]{1,0:T(8,128)(2,1)S(1)}) custom-call(bf16[224,512]{1,0:T(8,128)(2,1)S(1)} %get-tuple-element.33.placed_ref, bf16[512,2048]{1,0:T(8,128)(2,1)S(1)} %get-tuple-element.31.wd_ref), custom_call_target="tpu_custom_call" | custom-call | flops 603979776 | bytes 2097152 | tf_op jit(solution)/shard_map/pallas_call | solution.py:313
  26.9 0.5 %collective-permute-start.11 = (bf16[64,2048]{1,0:T(8,128)(2,1)S(1)}, bf16[64,2048]{1,0:T(8,128)(2,1)S(1)}, u32[]{:S(2)}, u32[]{:S(2)}) collective-permute-start(bf16[64,2048]{1,0:T(8,128)(2,1)S(1)} %get-tuple-element.39), channel_id=1, source_target_pairs={{0,1},{1,0},{2,3},{3,2},{4,5},{5,4},{6,7},{7,6},{8,9},{9,8},{10,11... | collective-permute-start | bytes 786440 | tf_op jit(solution)/shard_map/ppermute | solution.py:355
  27.8 3.6 %collective-permute-start.10 = (bf16[32,2048]{1,0:T(8,128)(2,1)S(1)}, bf16[32,2048]{1,0:T(8,128)(2,1)S(1)}, u32[]{:S(2)}, u32[]{:S(2)}) collective-permute-start(bf16[32,2048]{1,0:T(8,128)(2,1)S(1)} %get-tuple-element.37), channel_id=1, source_target_pairs={{0,14},{1,13},{2,12},{3,15},{4,10},{5,9},{6,8},{7,11},{8,6},{9,5},... | collective-permute-start | bytes 393224 | tf_op jit(solution)/shard_map/ppermute | solution.py:351
  31.5 0.7 %collective-permute-start.14 = (bf16[32,2048]{1,0:T(8,128)(2,1)S(1)}, bf16[32,2048]{1,0:T(8,128)(2,1)S(1)}, u32[]{:S(2)}, u32[]{:S(2)}) collective-permute-start(bf16[32,2048]{1,0:T(8,128)(2,1)S(1)} %get-tuple-element.40), channel_id=1, source_target_pairs={{1,3},{3,1},{5,7},{7,5},{9,11},{11,9},{13,15},{15,13},{17,19},{19,... | collective-permute-start | bytes 393224 | tf_op jit(solution)/shard_map/ppermute | solution.py:351
  32.2 1.8 %collective-permute-start.12 = (bf16[32,2048]{1,0:T(8,128)(2,1)S(1)}, bf16[32,2048]{1,0:T(8,128)(2,1)S(1)}, u32[]{:S(2)}, u32[]{:S(2)}) collective-permute-start(bf16[32,2048]{1,0:T(8,128)(2,1)S(1)} %get-tuple-element.46), channel_id=1, source_target_pairs={{0,8},{1,11},{2,10},{3,9},{4,12},{5,15},{6,14},{7,13},{8,0},{9,3},... | collective-permute-start | bytes 393224 | tf_op jit(solution)/shard_map/ppermute | solution.py:351
  34.0 1.1 %shard_map.144 = (bf16[16,2048]{1,0:T(8,128)(2,1)S(1)}, f32[16,4,1024]{2,1,0:T(4,128)S(1)}, f32[16,4,1024]{2,1,0:T(4,128)S(1)}) custom-call(s32[16]{0:T(128)S(1)} %copy-done.7, s32[2,288]{1,0:T(2,128)S(1)} %copy-done.6, bf16[6,16,1024]{2,1,0:T(8,128)(2,1)S(1)} %bitcast.8, f32[4,1024]{1,0:T(4,128)S(1)} %copy-done.5, f32[7,1024]{1,0:T(8,128)S(1)} %copy-done.4, ...), custom_call_target="tpu_custom_call" | custom-call | flops 18874368 | bytes 1179648 | tf_op jit(solution)/shard_map/pallas_call | solution.py:313
  35.1 1.9 %collective-permute-done.10 = bf16[32,2048]{1,0:T(8,128)(2,1)S(1)} collective-permute-done((bf16[32,2048]{1,0:T(8,128)(2,1)S(1)}, bf16[32,2048]{1,0:T(8,128)(2,1)S(1)}, u32[]{:S(2)}, u32[]{:S(2)}) %collective-permute-start.10) | collective-permute-done | bytes 131104 | tf_op jit(solution)/shard_map/ppermute | solution.py:351
  37.0 4.6 %collective-permute-done.13 = bf16[32,2048]{1,0:T(8,128)(2,1)S(1)} collective-permute-done((bf16[32,2048]{1,0:T(8,128)(2,1)S(1)}, bf16[32,2048]{1,0:T(8,128)(2,1)S(1)}, u32[]{:S(2)}, u32[]{:S(2)}) %collective-permute-start.13) | collective-permute-done | bytes 131104 | tf_op jit(solution)/shard_map/ppermute | solution.py:351
  41.6 0.5 %collective-permute-done.12 = bf16[32,2048]{1,0:T(8,128)(2,1)S(1)} collective-permute-done((bf16[32,2048]{1,0:T(8,128)(2,1)S(1)}, bf16[32,2048]{1,0:T(8,128)(2,1)S(1)}, u32[]{:S(2)}, u32[]{:S(2)}) %collective-permute-start.12) | collective-permute-done | bytes 131104 | tf_op jit(solution)/shard_map/ppermute | solution.py:351
  42.4 1.0 %collective-permute-done.15.got_ref = bf16[16,2048]{1,0:T(8,128)(2,1)S(1)} collective-permute-done((bf16[16,2048]{1,0:T(8,128)(2,1)S(1)}, bf16[16,2048]{1,0:T(8,128)(2,1)S(1)}, u32[]{:S(2)}, u32[]{:S(2)}) %collective-permute-start.15) | collective-permute-done | bytes 65568 | tf_op jit(solution)/shard_map/ppermute | solution.py:355
  43.4 1.6 %shard_map.145 = bf16[16,4,1024]{2,1,0:T(4,128)(2,1)} custom-call(f32[32,2048]{1,0:T(8,128)S(1)} %convert_add_fusion.mine_ref, bf16[16,2048]{1,0:T(8,128)(2,1)S(1)} %collective-permute-done.15.got_ref, bf16[16,2048]{1,0:T(8,128)(2,1)S(1)} %get-tuple-element.48.rest_ref, bf16[2048,1024]{1,0:T(8,128)(2,1)S(1)} %copy-done.1, ...), custom_call_target="tpu_custom_call" | custom-call | tf_op jit(solution)/shard_map/pallas_call | solution.py:313
  (36 shorter events, 2.2 us)
Async XLA Ops:
  1.0 1.5 %collective-permute-start = (bf16[16,2176]{1,0:T(8,128)(2,1)S(1)}, bf16[16,2176]{1,0:T(8,128)(2,1)S(1)}, u32[]{:S(2)}, u32[]{:S(2)}) collective-permute-start(bf16[16,2176]{1,0:T(8,128)(2,1)S(1)} %shard_map.136.own_ref), channel_id=1, source_target_pairs={{0,1},{1,0},{2,3},{3,2},{4,5},{5,4},{6,7},{7,6},{8,9},{9,8},{10,11... | collective-permute-start | bytes 208904 | tf_op jit(solution)/shard_map/ppermute | solution.py:355
  2.5 8.7 %collective-permute-start.2 = (bf16[32,2176]{1,0:T(8,128)(2,1)S(1)}, bf16[32,2176]{1,0:T(8,128)(2,1)S(1)}, u32[]{:S(2)}, u32[]{:S(2)}) collective-permute-start(bf16[32,2176]{1,0:T(8,128)(2,1)S(1)} %shard_map.137.refs_0_), channel_id=1, source_target_pairs={{1,3},{3,1},{5,7},{7,5},{9,11},{11,9},{13,15},{15,13},{17,19},{19,... | collective-permute-start | bytes 417800 | tf_op jit(solution)/shard_map/ppermute | solution.py:351
  3.2 9.3 %collective-permute-start.1 = (bf16[32,2176]{1,0:T(8,128)(2,1)S(1)}, bf16[32,2176]{1,0:T(8,128)(2,1)S(1)}, u32[]{:S(2)}, u32[]{:S(2)}) collective-permute-start(bf16[32,2176]{1,0:T(8,128)(2,1)S(1)} %shard_map.137.refs_0_), channel_id=1, source_target_pairs={{0,12},{1,15},{2,14},{3,13},{4,8},{5,11},{6,10},{7,9},{8,4},{9,7},... | collective-permute-start | bytes 417800 | tf_op jit(solution)/shard_map/ppermute | solution.py:351
  8.2 7.4 %collective-permute-start.6 = (bf16[32,2176]{1,0:T(8,128)(2,1)S(1)}, bf16[32,2176]{1,0:T(8,128)(2,1)S(1)}, u32[]{:S(2)}, u32[]{:S(2)}) collective-permute-start(bf16[32,2176]{1,0:T(8,128)(2,1)S(1)} %shard_map.137.refs_0_), channel_id=1, source_target_pairs={{0,6},{1,11},{2,4},{3,9},{4,2},{5,15},{6,0},{7,13},{8,14},{9,3},{1... | collective-permute-start | bytes 417800 | tf_op jit(solution)/shard_map/ppermute | solution.py:351
  8.7 11.8 %collective-permute-start.5 = (bf16[32,2176]{1,0:T(8,128)(2,1)S(1)}, bf16[32,2176]{1,0:T(8,128)(2,1)S(1)}, u32[]{:S(2)}, u32[]{:S(2)}) collective-permute-start(bf16[32,2176]{1,0:T(8,128)(2,1)S(1)} %shard_map.137.refs_0_), channel_id=1, source_target_pairs={{0,4},{1,9},{2,6},{3,11},{4,0},{5,13},{6,2},{7,15},{8,12},{9,1},{1... | collective-permute-start | bytes 417800 | tf_op jit(solution)/shard_map/ppermute | solution.py:351
  11.2 12.1 %collective-permute-start.4 = (bf16[32,2176]{1,0:T(8,128)(2,1)S(1)}, bf16[32,2176]{1,0:T(8,128)(2,1)S(1)}, u32[]{:S(2)}, u32[]{:S(2)}) collective-permute-start(bf16[32,2176]{1,0:T(8,128)(2,1)S(1)} %collective-permute-done.2.refs_2_), channel_id=1, source_target_pairs={{1,0},{3,2},{5,4},{7,6},{9,8},{11,10},{13,12},{15,14},{17,16},{19,... | collective-permute-start | bytes 417800 | tf_op jit(solution)/shard_map/ppermute | solution.py:355
  12.5 10.9 %collective-permute-start.3 = (bf16[32,2176]{1,0:T(8,128)(2,1)S(1)}, bf16[32,2176]{1,0:T(8,128)(2,1)S(1)}, u32[]{:S(2)}, u32[]{:S(2)}) collective-permute-start(bf16[32,2176]{1,0:T(8,128)(2,1)S(1)} %collective-permute-done.1.refs_1_), channel_id=1, source_target_pairs={{0,1},{1,0},{2,3},{3,2},{4,5},{5,4},{6,7},{7,6},{8,9},{9,8},{10,11... | collective-permute-start | bytes 417800 | tf_op jit(solution)/shard_map/ppermute | solution.py:355
  15.6 9.1 %collective-permute-start.8 = (bf16[32,2176]{1,0:T(8,128)(2,1)S(1)}, bf16[32,2176]{1,0:T(8,128)(2,1)S(1)}, u32[]{:S(2)}, u32[]{:S(2)}) collective-permute-start(bf16[32,2176]{1,0:T(8,128)(2,1)S(1)} %collective-permute-done.6.refs_1_.refs_6_), channel_id=1, source_target_pairs={{0,1},{1,0},{2,3},{3,2},{4,5},{5,4},{6,7},{7,6},{8,9},{9,8},{10,11... | collective-permute-start | bytes 417800 | tf_op jit(solution)/shard_map/ppermute | solution.py:355
  20.5 4.2 %collective-permute-start.7 = (bf16[32,2176]{1,0:T(8,128)(2,1)S(1)}, bf16[32,2176]{1,0:T(8,128)(2,1)S(1)}, u32[]{:S(2)}, u32[]{:S(2)}) collective-permute-start(bf16[32,2176]{1,0:T(8,128)(2,1)S(1)} %collective-permute-done.5.refs_0_.refs_5_), channel_id=1, source_target_pairs={{0,1},{1,0},{2,3},{3,2},{4,5},{5,4},{6,7},{7,6},{8,9},{9,8},{10,11... | collective-permute-start | bytes 417800 | tf_op jit(solution)/shard_map/ppermute | solution.py:355
  20.9 2.9 %copy-start = (bf16[1,2048,512]{2,1,0:T(8,128)(2,1)S(1)}, bf16[1,2048,512]{2,1,0:T(8,128)(2,1)}, u32[]{:S(2)}) copy-start(bf16[1,2048,512]{2,1,0:T(8,128)(2,1)} %param.17) | copy-start | bytes 6291460
  23.8 0.9 %copy-start.3 = (s32[288,2]{1,0:T(8,128)S(1)}, s32[288,2]{1,0:T(8,128)}, u32[]{:S(2)}) copy-start(s32[288,2]{1,0:T(8,128)} %constant.5.clone.target_ref) | copy-start | bytes 6916
  23.8 0.9 %copy-start.6 = (s32[2,288]{1,0:T(2,128)S(1)}, s32[2,288]{1,0:T(2,128)}, u32[]{:S(2)}) copy-start(s32[2,288]{1,0:T(2,128)} %constant.4.clone.table_ref) | copy-start | bytes 6916
  26.1 7.9 %copy-start.2 = (bf16[16,6,1024]{2,0,1:T(8,128)(2,1)S(1)}, bf16[16,6,1024]{2,0,1:T(8,128)(2,1)}, u32[]{:S(2)}) copy-start(bf16[16,6,1024]{2,0,1:T(8,128)(2,1)} %param.23) | copy-start | bytes 589828
  26.1 7.9 %copy-start.4 = (f32[7,1024]{1,0:T(8,128)S(1)}, f32[7,1024]{1,0:T(8,128)}, u32[]{:S(2)}) copy-start(f32[7,1024]{1,0:T(8,128)} %conv_ref.1) | copy-start | bytes 86020
  26.1 7.9 %copy-start.5 = (f32[4,1024]{1,0:T(4,128)S(1)}, f32[4,1024]{1,0:T(4,128)}, u32[]{:S(2)}) copy-start(f32[4,1024]{1,0:T(4,128)} %offset_ref.1) | copy-start | bytes 49156
  26.1 7.9 %copy-start.7 = (s32[16]{0:T(128)S(1)}, s32[16]{0:T(128)}, u32[]{:S(2)}) copy-start(s32[16]{0:T(128)} %count_ref.1) | copy-start | bytes 196
  26.1 1.6 %collective-permute-start.9 = (bf16[64,2048]{1,0:T(8,128)(2,1)S(1)}, bf16[64,2048]{1,0:T(8,128)(2,1)S(1)}, u32[]{:S(2)}, u32[]{:S(2)}) collective-permute-start(bf16[64,2048]{1,0:T(8,128)(2,1)S(1)} %get-tuple-element.36), channel_id=1, source_target_pairs={{0,1},{1,0},{2,3},{3,2},{4,5},{5,4},{6,7},{7,6},{8,9},{9,8},{10,11... | collective-permute-start | bytes 786440 | tf_op jit(solution)/shard_map/ppermute | solution.py:355
  26.3 17.2 %copy-start.1 = (bf16[2048,1024]{1,0:T(8,128)(2,1)S(1)}, bf16[2048,1024]{1,0:T(8,128)(2,1)}, u32[]{:S(2)}) copy-start(bf16[2048,1024]{1,0:T(8,128)(2,1)} %proj_ref.1) | copy-start | bytes 12582916
  26.9 4.5 %collective-permute-start.11 = (bf16[64,2048]{1,0:T(8,128)(2,1)S(1)}, bf16[64,2048]{1,0:T(8,128)(2,1)S(1)}, u32[]{:S(2)}, u32[]{:S(2)}) collective-permute-start(bf16[64,2048]{1,0:T(8,128)(2,1)S(1)} %get-tuple-element.39), channel_id=1, source_target_pairs={{0,1},{1,0},{2,3},{3,2},{4,5},{5,4},{6,7},{7,6},{8,9},{9,8},{10,11... | collective-permute-start | bytes 786440 | tf_op jit(solution)/shard_map/ppermute | solution.py:355
  27.8 9.2 %collective-permute-start.10 = (bf16[32,2048]{1,0:T(8,128)(2,1)S(1)}, bf16[32,2048]{1,0:T(8,128)(2,1)S(1)}, u32[]{:S(2)}, u32[]{:S(2)}) collective-permute-start(bf16[32,2048]{1,0:T(8,128)(2,1)S(1)} %get-tuple-element.37), channel_id=1, source_target_pairs={{0,14},{1,13},{2,12},{3,15},{4,10},{5,9},{6,8},{7,11},{8,6},{9,5},... | collective-permute-start | bytes 393224 | tf_op jit(solution)/shard_map/ppermute | solution.py:351
  31.5 10.1 %collective-permute-start.13 = (bf16[32,2048]{1,0:T(8,128)(2,1)S(1)}, bf16[32,2048]{1,0:T(8,128)(2,1)S(1)}, u32[]{:S(2)}, u32[]{:S(2)}) collective-permute-start(bf16[32,2048]{1,0:T(8,128)(2,1)S(1)} %get-tuple-element.47), channel_id=1, source_target_pairs={{0,6},{1,5},{2,4},{3,7},{4,2},{5,1},{6,0},{7,3},{8,14},{9,13},{10,... | collective-permute-start | bytes 393224 | tf_op jit(solution)/shard_map/ppermute | solution.py:351
  31.5 10.0 %collective-permute-start.14 = (bf16[32,2048]{1,0:T(8,128)(2,1)S(1)}, bf16[32,2048]{1,0:T(8,128)(2,1)S(1)}, u32[]{:S(2)}, u32[]{:S(2)}) collective-permute-start(bf16[32,2048]{1,0:T(8,128)(2,1)S(1)} %get-tuple-element.40), channel_id=1, source_target_pairs={{1,3},{3,1},{5,7},{7,5},{9,11},{11,9},{13,15},{15,13},{17,19},{19,... | collective-permute-start | bytes 393224 | tf_op jit(solution)/shard_map/ppermute | solution.py:351
  32.2 9.8 %collective-permute-start.12 = (bf16[32,2048]{1,0:T(8,128)(2,1)S(1)}, bf16[32,2048]{1,0:T(8,128)(2,1)S(1)}, u32[]{:S(2)}, u32[]{:S(2)}) collective-permute-start(bf16[32,2048]{1,0:T(8,128)(2,1)S(1)} %get-tuple-element.46), channel_id=1, source_target_pairs={{0,8},{1,11},{2,10},{3,9},{4,12},{5,15},{6,14},{7,13},{8,0},{9,3},... | collective-permute-start | bytes 393224 | tf_op jit(solution)/shard_map/ppermute | solution.py:351
  42.1 1.3 %collective-permute-start.15 = (bf16[16,2048]{1,0:T(8,128)(2,1)S(1)}, bf16[16,2048]{1,0:T(8,128)(2,1)S(1)}, u32[]{:S(2)}, u32[]{:S(2)}) collective-permute-start(bf16[16,2048]{1,0:T(8,128)(2,1)S(1)} %slice.7), channel_id=1, source_target_pairs={{0,1},{1,0},{2,3},{3,2},{4,5},{5,4},{6,7},{7,6},{8,9},{9,8},{10,11... | collective-permute-start | bytes 196616 | tf_op jit(solution)/shard_map/ppermute | solution.py:355

commit v2 on v1

--- a/solution.py
+++ b/solution.py
@@ -286,21 +286,14 @@
     return [pl.BlockSpec(memory_space=pltpu.VMEM)] * count
 
 
-def gather_partners(chips):
-    between = list(range(2, chips - 2))
-    half = len(between) // 2
-    return [
-        [chips - 2, None] + between[:half],
-        [chips - 1, 1] + between[half:],
-    ]
+def gather_partners(chips, across):
+    others = [m for m in range(1, chips) if m != across]
+    return [others[-2:-1] + others[:-2][0::2], others[-1:] + others[:-2][1::2]]
 
 
 def reduce_partners(chips):
-    masks = list(range(chips - 1, 0, -1)) + [None]
-    return [
-        [m for k, m in enumerate(masks) if k % 4 in (0, 3)],
-        [m for k, m in enumerate(masks) if k % 4 in (1, 2)],
-    ]
+    evens = sorted(range(2, chips, 2), key=lambda m: (m != chips // 2, m))
+    return [[m + 1 for m in evens] + [None], evens + [1]]
 
 
 def in_hbm(x):
@@ -340,9 +333,10 @@
     hidden = w_gate.shape[2]
     talker_width = talker_proj.shape[1]
     horizon = frame_offset.shape[0]
-    lists = gather_partners(devices // 2)
+    across = devices // 4
+    lists = gather_partners(devices // 2, across)
     back = reduce_partners(devices // 2)
-    slots = len(lists[0])
+    slots = len(back[0])
     width = -(-3 * devices // LANES) * LANES
     bf16 = functools.partial(jax.ShapeDtypeStruct, dtype=jnp.bfloat16)
 
@@ -350,9 +344,11 @@
         pairs = [(i, i ^ (chips[i % 2][j] * 2)) for i in range(devices) if chips[i % 2][j]]
         return lax.ppermute(x, "ep", pairs)
 
-    def near(x, j=None):
-        pairs = [(i, i ^ 1) for i in range(devices) if j is None or lists[i % 2][j]]
-        return lax.ppermute(x, "ep", pairs)
+    def near(x):
+        return lax.ppermute(x, "ep", [(i, i ^ 1) for i in range(devices)])
+
+    def both_cores(x):
+        return lax.ppermute(x, "ep", [(i, i ^ (2 * across)) for i in range(devices)])
 
     def side(chips, flip):
         blocks = [[-1, -1] if m is None else [2 * m + flip, 2 * m + 1 - flip] for m in chips]
@@ -361,16 +357,14 @@
     def spread(blocks):
         return np.repeat(np.array(blocks, np.int32), rows)
 
-    first_slots, last_slots = range(slots // 2), range(slots // 2, slots)
-
-    def arriving(c, chosen):
-        some = [[chips[j] for j in chosen] for chips in (lists[c], lists[1 - c])]
-        return side(some[0], 0) + side(some[1], 1)
+    def arriving(c):
+        ours, theirs = lists[c], lists[1 - c]
+        blocks = [0, 1, 2 * across, 2 * across + 1]
+        blocks += side(ours[:-1], 0) + side(theirs[:-1], 1)
+        return spread(blocks + side(ours[-1:], 0) + side(theirs[-1:], 1))
 
     half = slots // 2
-    table = np.stack(
-        [spread([0, 1] + arriving(c, first_slots) + arriving(c, last_slots)) for c in range(2)]
-    )
+    table = np.stack([arriving(c) for c in range(2)])
     keep_to = np.stack([spread(side(back[c], 0) + [0, 1]) for c in range(2)], axis=1)
     give_to = np.stack([spread(side(back[1 - c], 1)) for c in range(2)], axis=1)
     cut = 2 * rows * half
@@ -382,9 +376,10 @@
         [in_hbm(v) for v in (thinker_rows, expert_ids.T, gate_weights.T, talker_slot)],
         megabytes=4,
     )
-    pair = call(pair_kernel, bf16((2 * rows, features + width)), [own, near(own)])
-    pair, w_up, w_down = lax.optimization_barrier((pair, w_up, w_down))
-    mine = [far(pair, lists, j) for j in range(slots)]
+    other = near(own)
+    opposite = both_cores(own)
+    pair = call(pair_kernel, bf16((2 * rows, features + width)), [own, other])
+    mine = [far(pair, lists, j) for j in range(len(lists[0]))]
     w_up_here, w_down_here = call(
         fetch_kernel,
         [bf16(w_up.shape[1:]), bf16(w_down.shape[1:])],
@@ -393,7 +388,8 @@
         scratch=[pltpu.SemaphoreType.DMA((2,))],
         cost=pl.CostEstimate(flops=0, bytes_accessed=4 * w_up.size, transcendentals=0),
     )
-    early_parts = [pair] + [mine[j] for j in first_slots] + [near(mine[j], j) for j in first_slots]
+    theirs = [near(m) for m in mine]
+    early_parts = [pair, opposite, near(opposite)] + mine[:-1] + theirs[:-1]
     early_rows = sum(p.shape[0] for p in early_parts)
     early = call(
         functools.partial(early_kernel, devices),
@@ -407,8 +403,7 @@
             transcendentals=0,
         ),
     )
-    late_parts = [mine[j] for j in last_slots]
-    late_parts += [near(mine[j], j) for j in last_slots]
+    late_parts = [mine[-1], theirs[-1]]
     late_rows = sum(p.shape[0] for p in late_parts)
     parts = early_parts + late_parts
     total = early_rows + late_rows

time: 45.2 us -> 47 us (1.040)
  waiting for transfers between devices: 9.37 us -> 20.1 us
  starting transfers between devices: 25.8 us -> 16.8 us
    ppermute x8 -> x9, starting transfers between devices: 11 us -> 4.26 us  [the longest x8 3.76 us: near(): return lax.ppermute(x, 'ep', [(i, i ^ 1) for i in range(devices)])]
    ppermute x8 -> x9, waiting for transfers between devices: 2.21 us -> 8.29 us  [the longest x1 5.72 us: both_cores(): return lax.ppermute(x, 'ep', [(i, i ^ 2 * across) for i in range(devices)])]
    ppermute x8 -> x7, waiting for transfers between devices: 7.16 us -> 11.8 us  [far(): return lax.ppermute(x, 'ep', pairs)]
    ppermute x8 -> x7, starting transfers between devices: 14.8 us -> 12.5 us  [far(): return lax.ppermute(x, 'ep', pairs)]
  transfers between devices with their start and end apart: 16 -> 16, of which waited for: 7 -> 8; matrix products, arithmetic and copies ran while one was open for 0% -> 0% of each run, Pallas kernels for 11% -> 11%
where the time goes in v2:
time: 47 us; the launch traced here: 46.8 us
  waiting for transfers between devices  20.1 us (43%)
  starting transfers between devices  16.8 us (36%)
  Pallas kernels  9.23 us (20%)
    ppermute x7, starting transfers between devices, far(): return lax.ppermute(x, 'ep', pairs)  12.5 us
    ppermute x7, waiting for transfers between devices, far(): return lax.ppermute(x, 'ep', pairs)  11.8 us
    pallas_call x10, Pallas kernels, call(): pl.pallas_call(kernel, out_shape=out_shape, in_specs=in_specs or specs, o...  9.23 us
    ppermute x1, waiting for transfers between devices, both_cores(): return lax.ppermute(x, 'ep', [(i, i ^ 2 * across) for i in range(devices)])  5.72 us
    ppermute x8, starting transfers between devices, near(): return lax.ppermute(x, 'ep', [(i, i ^ 1) for i in range(devices)])  3.76 us
    ppermute x8, waiting for transfers between devices, near(): return lax.ppermute(x, 'ep', [(i, i ^ 1) for i in range(devices)])  2.57 us
  transfers between devices with their start and end apart: 16, of which 8 were waited for; matrix products, arithmetic and copies ran while one was open for 0% of the time, Pallas kernels for 11%

profile of v2, /device:TPU:0, one launch (start us, length us, event | category | flops | bytes accessed | tf_op | source)
XLA Modules:
  0.0 46.8 jit_solution(17627074396222991619)
XLA Ops:
  0.0 1.0 %shard_map.137.own_ref = bf16[16,2176]{1,0:T(8,128)(2,1)S(1)} custom-call(bf16[16,2048]{1,0:T(8,128)(2,1)} %rows_ref.1, s32[8,16]{1,0:T(8,128)} %bitcast.11, f32[8,16]{1,0:T(8,128)} %bitcast.12, s32[1,16]{1,0:T(1,128)} %slot_ref.1), custom_call_target="tpu_custom_call" | custom-call | tf_op jit(solution)/shard_map/pallas_call | solution.py:306
  1.0 0.6 %collective-permute-start = (bf16[16,2176]{1,0:T(8,128)(2,1)S(1)}, bf16[16,2176]{1,0:T(8,128)(2,1)S(1)}, u32[]{:S(2)}, u32[]{:S(2)}) collective-permute-start(bf16[16,2176]{1,0:T(8,128)(2,1)S(1)} %shard_map.137.own_ref), channel_id=1, source_target_pairs={{0,1},{1,0},{2,3},{3,2},{4,5},{5,4},{6,7},{7,6},{8,9},{9,8},{10,11... | collective-permute-start | bytes 208904 | tf_op jit(solution)/shard_map/ppermute | solution.py:348
  1.6 0.9 %collective-permute-done.other_ref = bf16[16,2176]{1,0:T(8,128)(2,1)S(1)} collective-permute-done((bf16[16,2176]{1,0:T(8,128)(2,1)S(1)}, bf16[16,2176]{1,0:T(8,128)(2,1)S(1)}, u32[]{:S(2)}, u32[]{:S(2)}) %collective-permute-start) | collective-permute-done | bytes 69664 | tf_op jit(solution)/shard_map/ppermute | solution.py:348
  2.5 2.9 %collective-permute-start.4 = (bf16[32,2176]{1,0:T(8,128)(2,1)S(1)}, bf16[32,2176]{1,0:T(8,128)(2,1)S(1)}, u32[]{:S(2)}, u32[]{:S(2)}) collective-permute-start(bf16[32,2176]{1,0:T(8,128)(2,1)S(1)} %shard_map.138.refs_0_), channel_id=1, source_target_pairs={{0,2},{1,5},{2,0},{3,7},{4,6},{5,1},{6,4},{7,3},{8,10},{9,13},{10,... | collective-permute-start | bytes 417800 | tf_op jit(solution)/shard_map/ppermute | solution.py:345
  5.4 3.6 %collective-permute-start.3 = (bf16[32,2176]{1,0:T(8,128)(2,1)S(1)}, bf16[32,2176]{1,0:T(8,128)(2,1)S(1)}, u32[]{:S(2)}, u32[]{:S(2)}) collective-permute-start(bf16[32,2176]{1,0:T(8,128)(2,1)S(1)} %shard_map.138.refs_0_), channel_id=1, source_target_pairs={{0,12},{1,15},{2,14},{3,13},{4,8},{5,11},{6,10},{7,9},{8,4},{9,7},... | collective-permute-start | bytes 417800 | tf_op jit(solution)/shard_map/ppermute | solution.py:345
  9.0 0.5 %collective-permute-start.1 = (bf16[16,2176]{1,0:T(8,128)(2,1)S(1)}, bf16[16,2176]{1,0:T(8,128)(2,1)S(1)}, u32[]{:S(2)}, u32[]{:S(2)}) collective-permute-start(bf16[16,2176]{1,0:T(8,128)(2,1)S(1)} %shard_map.137.own_ref), channel_id=1, source_target_pairs={{0,8},{1,9},{2,10},{3,11},{4,12},{5,13},{6,14},{7,15},{8,0},{9,1},... | collective-permute-start | bytes 208904 | tf_op jit(solution)/shard_map/ppermute | solution.py:351
  9.5 1.3 %collective-permute-start.6 = (bf16[32,2176]{1,0:T(8,128)(2,1)S(1)}, bf16[32,2176]{1,0:T(8,128)(2,1)S(1)}, u32[]{:S(2)}, u32[]{:S(2)}) collective-permute-start(bf16[32,2176]{1,0:T(8,128)(2,1)S(1)} %collective-permute-done.4.refs_4_), channel_id=1, source_target_pairs={{0,1},{1,0},{2,3},{3,2},{4,5},{5,4},{6,7},{7,6},{8,9},{9,8},{10,11... | collective-permute-start | bytes 417800 | tf_op jit(solution)/shard_map/ppermute | solution.py:348
  10.8 3.1 %collective-permute-done.3.refs_3_ = bf16[32,2176]{1,0:T(8,128)(2,1)S(1)} collective-permute-done((bf16[32,2176]{1,0:T(8,128)(2,1)S(1)}, bf16[32,2176]{1,0:T(8,128)(2,1)S(1)}, u32[]{:S(2)}, u32[]{:S(2)}) %collective-permute-start.3) | collective-permute-done | bytes 139296 | tf_op jit(solution)/shard_map/ppermute | solution.py:345
  13.9 0.7 %collective-permute-start.5 = (bf16[32,2176]{1,0:T(8,128)(2,1)S(1)}, bf16[32,2176]{1,0:T(8,128)(2,1)S(1)}, u32[]{:S(2)}, u32[]{:S(2)}) collective-permute-start(bf16[32,2176]{1,0:T(8,128)(2,1)S(1)} %collective-permute-done.3.refs_3_), channel_id=1, source_target_pairs={{0,1},{1,0},{2,3},{3,2},{4,5},{5,4},{6,7},{7,6},{8,9},{9,8},{10,11... | collective-permute-start | bytes 417800 | tf_op jit(solution)/shard_map/ppermute | solution.py:348
  14.6 5.7 %collective-permute-done.1.refs_1_ = bf16[16,2176]{1,0:T(8,128)(2,1)S(1)} collective-permute-done((bf16[16,2176]{1,0:T(8,128)(2,1)S(1)}, bf16[16,2176]{1,0:T(8,128)(2,1)S(1)}, u32[]{:S(2)}, u32[]{:S(2)}) %collective-permute-start.1) | collective-permute-done | bytes 69664 | tf_op jit(solution)/shard_map/ppermute | solution.py:351
  20.8 2.4 %shard_map.136 = (bf16[2048,512]{1,0:T(8,128)(2,1)S(1)}, bf16[512,2048]{1,0:T(8,128)(2,1)S(1)}) custom-call(bf16[2048,512]{1,0:T(8,128)(2,1)} %bitcast.9, bf16[512,2048]{1,0:T(8,128)(2,1)} %bitcast.10), custom_call_target="tpu_custom_call" | custom-call | bytes 4194304 | tf_op jit(solution)/shard_map/pallas_call | solution.py:306
  23.2 0.4 copy-done
  23.7 1.0 %shard_map.139.early_ref = bf16[192,512]{1,0:T(8,128)(2,1)S(1)} custom-call(bf16[2048,512]{1,0:T(8,128)(2,1)S(1)} %bitcast.6, bf16[2048,512]{1,0:T(8,128)(2,1)S(1)} %get-tuple-element.25.wu_ref, bf16[32,2176]{1,0:T(8,128)(2,1)S(1)} %shard_map.138.refs_0_, bf16[16,2176]{1,0:T(8,128)(2,1)S(1)} %collective-permute-done.1.refs_1_, ...), custom_call_target="tpu_custom_call" | custom-call | flops 805306368 | bytes 4194304 | tf_op jit(solution)/shard_map/pallas_call | solution.py:306
  24.8 1.4 %shard_map.140 = (bf16[64,2048]{1,0:T(8,128)(2,1)S(1)}, bf16[224,512]{1,0:T(8,128)(2,1)S(1)}) custom-call(s32[2,256]{1,0:T(2,128)S(1)} %copy-done.6, s32[288,2]{1,0:T(8,128)S(1)} %copy-done.3, bf16[2048,512]{1,0:T(8,128)(2,1)S(1)} %bitcast.7, bf16[2048,512]{1,0:T(8,128)(2,1)S(1)} %get-tuple-element.25.wu_ref, ...), custom_call_target="tpu_custom_call" | custom-call | tf_op jit(solution)/shard_map/pallas_call | solution.py:306
  26.6 0.6 %shard_map.141 = (bf16[64,2048]{1,0:T(8,128)(2,1)S(1)}, bf16[64,2048]{1,0:T(8,128)(2,1)S(1)}, bf16[64,2048]{1,0:T(8,128)(2,1)S(1)}, bf16[32,2048]{1,0:T(8,128)(2,1)S(1)}) custom-call(bf16[224,512]{1,0:T(8,128)(2,1)S(1)} %get-tuple-element.27.placed_ref, bf16[512,2048]{1,0:T(8,128)(2,1)S(1)} %get-tuple-element.26.wd_ref), custom_call_target="tpu_custom_call" | custom-call | flops 603979776 | bytes 2097152 | tf_op jit(solution)/shard_map/pallas_call | solution.py:306
  27.9 0.9 %collective-permute-start.10 = (bf16[32,2048]{1,0:T(8,128)(2,1)S(1)}, bf16[32,2048]{1,0:T(8,128)(2,1)S(1)}, u32[]{:S(2)}, u32[]{:S(2)}) collective-permute-start(bf16[32,2048]{1,0:T(8,128)(2,1)S(1)} %get-tuple-element.31), channel_id=1, source_target_pairs={{0,10},{1,9},{2,8},{3,11},{4,14},{5,13},{6,12},{7,15},{8,2},{9,1},... | collective-permute-start | bytes 393224 | tf_op jit(solution)/shard_map/ppermute | solution.py:345
  28.9 3.6 %collective-permute-start.13 = (bf16[32,2048]{1,0:T(8,128)(2,1)S(1)}, bf16[32,2048]{1,0:T(8,128)(2,1)S(1)}, u32[]{:S(2)}, u32[]{:S(2)}) collective-permute-start(bf16[32,2048]{1,0:T(8,128)(2,1)S(1)} %get-tuple-element.41), channel_id=1, source_target_pairs={{0,14},{1,13},{2,12},{3,15},{4,10},{5,9},{6,8},{7,11},{8,6},{9,5},... | collective-permute-start | bytes 393224 | tf_op jit(solution)/shard_map/ppermute | solution.py:345
  32.5 0.7 %collective-permute-start.14 = (bf16[32,2048]{1,0:T(8,128)(2,1)S(1)}, bf16[32,2048]{1,0:T(8,128)(2,1)S(1)}, u32[]{:S(2)}, u32[]{:S(2)}) collective-permute-start(bf16[32,2048]{1,0:T(8,128)(2,1)S(1)} %get-tuple-element.34), channel_id=1, source_target_pairs={{1,3},{3,1},{5,7},{7,5},{9,11},{11,9},{13,15},{15,13},{17,19},{19,... | collective-permute-start | bytes 393224 | tf_op jit(solution)/shard_map/ppermute | solution.py:345
  33.1 0.9 %collective-permute-start.12 = (bf16[32,2048]{1,0:T(8,128)(2,1)S(1)}, bf16[32,2048]{1,0:T(8,128)(2,1)S(1)}, u32[]{:S(2)}, u32[]{:S(2)}) collective-permute-start(bf16[32,2048]{1,0:T(8,128)(2,1)S(1)} %get-tuple-element.40), channel_id=1, source_target_pairs={{0,6},{1,5},{2,4},{3,7},{4,2},{5,1},{6,0},{7,3},{8,14},{9,13},{10,... | collective-permute-start | bytes 393224 | tf_op jit(solution)/shard_map/ppermute | solution.py:345
  34.1 1.0 %shard_map.144 = (bf16[16,2048]{1,0:T(8,128)(2,1)S(1)}, f32[16,4,1024]{2,1,0:T(4,128)S(1)}, f32[16,4,1024]{2,1,0:T(4,128)S(1)}) custom-call(s32[16]{0:T(128)S(1)} %copy-done.7, s32[2,256]{1,0:T(2,128)S(1)} %copy-done.6, bf16[6,16,1024]{2,1,0:T(8,128)(2,1)S(1)} %bitcast.8, f32[4,1024]{1,0:T(4,128)S(1)} %copy-done.5, f32[7,1024]{1,0:T(8,128)S(1)} %copy-done.4, ...), custom_call_target="tpu_custom_call" | custom-call | flops 16777216 | bytes 1048576 | tf_op jit(solution)/shard_map/pallas_call | solution.py:306
  35.1 6.1 %collective-permute-done.10 = bf16[32,2048]{1,0:T(8,128)(2,1)S(1)} collective-permute-done((bf16[32,2048]{1,0:T(8,128)(2,1)S(1)}, bf16[32,2048]{1,0:T(8,128)(2,1)S(1)}, u32[]{:S(2)}, u32[]{:S(2)}) %collective-permute-start.10) | collective-permute-done | bytes 131104 | tf_op jit(solution)/shard_map/ppermute | solution.py:345
  41.2 2.7 %collective-permute-done.12 = bf16[32,2048]{1,0:T(8,128)(2,1)S(1)} collective-permute-done((bf16[32,2048]{1,0:T(8,128)(2,1)S(1)}, bf16[32,2048]{1,0:T(8,128)(2,1)S(1)}, u32[]{:S(2)}, u32[]{:S(2)}) %collective-permute-start.12) | collective-permute-done | bytes 131104 | tf_op jit(solution)/shard_map/ppermute | solution.py:345
  44.0 1.2 %collective-permute-done.15.got_ref = bf16[16,2048]{1,0:T(8,128)(2,1)S(1)} collective-permute-done((bf16[16,2048]{1,0:T(8,128)(2,1)S(1)}, bf16[16,2048]{1,0:T(8,128)(2,1)S(1)}, u32[]{:S(2)}, u32[]{:S(2)}) %collective-permute-start.15) | collective-permute-done | bytes 65568 | tf_op jit(solution)/shard_map/ppermute | solution.py:348
  45.3 1.6 %shard_map.145 = bf16[16,4,1024]{2,1,0:T(4,128)(2,1)} custom-call(f32[32,2048]{1,0:T(8,128)S(1)} %convert_add_fusion.mine_ref, bf16[16,2048]{1,0:T(8,128)(2,1)S(1)} %collective-permute-done.15.got_ref, bf16[16,2048]{1,0:T(8,128)(2,1)S(1)} %get-tuple-element.42.rest_ref, bf16[2048,1024]{1,0:T(8,128)(2,1)S(1)} %copy-done.1, ...), custom_call_target="tpu_custom_call" | custom-call | tf_op jit(solution)/shard_map/pallas_call | solution.py:306
  (36 shorter events, 1.9 us)
Async XLA Ops:
  1.0 1.5 %collective-permute-start = (bf16[16,2176]{1,0:T(8,128)(2,1)S(1)}, bf16[16,2176]{1,0:T(8,128)(2,1)S(1)}, u32[]{:S(2)}, u32[]{:S(2)}) collective-permute-start(bf16[16,2176]{1,0:T(8,128)(2,1)S(1)} %shard_map.137.own_ref), channel_id=1, source_target_pairs={{0,1},{1,0},{2,3},{3,2},{4,5},{5,4},{6,7},{7,6},{8,9},{9,8},{10,11... | collective-permute-start | bytes 208904 | tf_op jit(solution)/shard_map/ppermute | solution.py:348
  2.5 7.0 %collective-permute-start.4 = (bf16[32,2176]{1,0:T(8,128)(2,1)S(1)}, bf16[32,2176]{1,0:T(8,128)(2,1)S(1)}, u32[]{:S(2)}, u32[]{:S(2)}) collective-permute-start(bf16[32,2176]{1,0:T(8,128)(2,1)S(1)} %shard_map.138.refs_0_), channel_id=1, source_target_pairs={{0,2},{1,5},{2,0},{3,7},{4,6},{5,1},{6,4},{7,3},{8,10},{9,13},{10,... | collective-permute-start | bytes 417800 | tf_op jit(solution)/shard_map/ppermute | solution.py:345
  5.4 8.5 %collective-permute-start.3 = (bf16[32,2176]{1,0:T(8,128)(2,1)S(1)}, bf16[32,2176]{1,0:T(8,128)(2,1)S(1)}, u32[]{:S(2)}, u32[]{:S(2)}) collective-permute-start(bf16[32,2176]{1,0:T(8,128)(2,1)S(1)} %shard_map.138.refs_0_), channel_id=1, source_target_pairs={{0,12},{1,15},{2,14},{3,13},{4,8},{5,11},{6,10},{7,9},{8,4},{9,7},... | collective-permute-start | bytes 417800 | tf_op jit(solution)/shard_map/ppermute | solution.py:345
  9.0 11.6 %collective-permute-start.7 = (bf16[32,2176]{1,0:T(8,128)(2,1)S(1)}, bf16[32,2176]{1,0:T(8,128)(2,1)S(1)}, u32[]{:S(2)}, u32[]{:S(2)}) collective-permute-start(bf16[32,2176]{1,0:T(8,128)(2,1)S(1)} %shard_map.138.refs_0_), channel_id=1, source_target_pairs={{0,6},{1,11},{2,4},{3,9},{4,2},{5,15},{6,0},{7,13},{8,14},{9,3},{1... | collective-permute-start | bytes 417800 | tf_op jit(solution)/shard_map/ppermute | solution.py:345
  9.0 11.3 %collective-permute-start.1 = (bf16[16,2176]{1,0:T(8,128)(2,1)S(1)}, bf16[16,2176]{1,0:T(8,128)(2,1)S(1)}, u32[]{:S(2)}, u32[]{:S(2)}) collective-permute-start(bf16[16,2176]{1,0:T(8,128)(2,1)S(1)} %shard_map.137.own_ref), channel_id=1, source_target_pairs={{0,8},{1,9},{2,10},{3,11},{4,12},{5,13},{6,14},{7,15},{8,0},{9,1},... | collective-permute-start | bytes 208904 | tf_op jit(solution)/shard_map/ppermute | solution.py:351
  9.5 13.7 %collective-permute-start.6 = (bf16[32,2176]{1,0:T(8,128)(2,1)S(1)}, bf16[32,2176]{1,0:T(8,128)(2,1)S(1)}, u32[]{:S(2)}, u32[]{:S(2)}) collective-permute-start(bf16[32,2176]{1,0:T(8,128)(2,1)S(1)} %collective-permute-done.4.refs_4_), channel_id=1, source_target_pairs={{0,1},{1,0},{2,3},{3,2},{4,5},{5,4},{6,7},{7,6},{8,9},{9,8},{10,11... | collective-permute-start | bytes 417800 | tf_op jit(solution)/shard_map/ppermute | solution.py:348
  13.9 9.4 %collective-permute-start.5 = (bf16[32,2176]{1,0:T(8,128)(2,1)S(1)}, bf16[32,2176]{1,0:T(8,128)(2,1)S(1)}, u32[]{:S(2)}, u32[]{:S(2)}) collective-permute-start(bf16[32,2176]{1,0:T(8,128)(2,1)S(1)} %collective-permute-done.3.refs_3_), channel_id=1, source_target_pairs={{0,1},{1,0},{2,3},{3,2},{4,5},{5,4},{6,7},{7,6},{8,9},{9,8},{10,11... | collective-permute-start | bytes 417800 | tf_op jit(solution)/shard_map/ppermute | solution.py:348
  20.3 2.9 %collective-permute-start.2 = (bf16[16,2176]{1,0:T(8,128)(2,1)S(1)}, bf16[16,2176]{1,0:T(8,128)(2,1)S(1)}, u32[]{:S(2)}, u32[]{:S(2)}) collective-permute-start(bf16[16,2176]{1,0:T(8,128)(2,1)S(1)} %collective-permute-done.1.refs_1_), channel_id=1, source_target_pairs={{0,1},{1,0},{2,3},{3,2},{4,5},{5,4},{6,7},{7,6},{8,9},{9,8},{10,11... | collective-permute-start | bytes 208904 | tf_op jit(solution)/shard_map/ppermute | solution.py:348
  20.6 4.1 %collective-permute-start.8 = (bf16[32,2176]{1,0:T(8,128)(2,1)S(1)}, bf16[32,2176]{1,0:T(8,128)(2,1)S(1)}, u32[]{:S(2)}, u32[]{:S(2)}) collective-permute-start(bf16[32,2176]{1,0:T(8,128)(2,1)S(1)} %collective-permute-done.7.refs_0_.refs_7_), channel_id=1, source_target_pairs={{0,1},{1,0},{2,3},{3,2},{4,5},{5,4},{6,7},{7,6},{8,9},{9,8},{10,11... | collective-permute-start | bytes 417800 | tf_op jit(solution)/shard_map/ppermute | solution.py:348
  20.8 2.9 %copy-start = (bf16[1,2048,512]{2,1,0:T(8,128)(2,1)S(1)}, bf16[1,2048,512]{2,1,0:T(8,128)(2,1)}, u32[]{:S(2)}) copy-start(bf16[1,2048,512]{2,1,0:T(8,128)(2,1)} %param.17) | copy-start | bytes 6291460
  23.7 1.1 %copy-start.3 = (s32[288,2]{1,0:T(8,128)S(1)}, s32[288,2]{1,0:T(8,128)}, u32[]{:S(2)}) copy-start(s32[288,2]{1,0:T(8,128)} %constant.5.clone.target_ref) | copy-start | bytes 6916
  23.7 1.1 %copy-start.6 = (s32[2,256]{1,0:T(2,128)S(1)}, s32[2,256]{1,0:T(2,128)}, u32[]{:S(2)}) copy-start(s32[2,256]{1,0:T(2,128)} %constant.4.clone.table_ref) | copy-start | bytes 6148
  26.2 7.9 %copy-start.2 = (bf16[16,6,1024]{2,0,1:T(8,128)(2,1)S(1)}, bf16[16,6,1024]{2,0,1:T(8,128)(2,1)}, u32[]{:S(2)}) copy-start(bf16[16,6,1024]{2,0,1:T(8,128)(2,1)} %param.23) | copy-start | bytes 589828
  26.2 7.9 %copy-start.4 = (f32[7,1024]{1,0:T(8,128)S(1)}, f32[7,1024]{1,0:T(8,128)}, u32[]{:S(2)}) copy-start(f32[7,1024]{1,0:T(8,128)} %conv_ref.1) | copy-start | bytes 86020
  26.2 7.9 %copy-start.5 = (f32[4,1024]{1,0:T(4,128)S(1)}, f32[4,1024]{1,0:T(4,128)}, u32[]{:S(2)}) copy-start(f32[4,1024]{1,0:T(4,128)} %offset_ref.1) | copy-start | bytes 49156
  26.2 7.8 %copy-start.7 = (s32[16]{0:T(128)S(1)}, s32[16]{0:T(128)}, u32[]{:S(2)}) copy-start(s32[16]{0:T(128)} %count_ref.1) | copy-start | bytes 196
  26.2 1.6 %collective-permute-start.9 = (bf16[64,2048]{1,0:T(8,128)(2,1)S(1)}, bf16[64,2048]{1,0:T(8,128)(2,1)S(1)}, u32[]{:S(2)}, u32[]{:S(2)}) collective-permute-start(bf16[64,2048]{1,0:T(8,128)(2,1)S(1)} %get-tuple-element.30), channel_id=1, source_target_pairs={{0,1},{1,0},{2,3},{3,2},{4,5},{5,4},{6,7},{7,6},{8,9},{9,8},{10,11... | collective-permute-start | bytes 786440 | tf_op jit(solution)/shard_map/ppermute | solution.py:348
  26.6 18.7 %copy-start.1 = (bf16[2048,1024]{1,0:T(8,128)(2,1)S(1)}, bf16[2048,1024]{1,0:T(8,128)(2,1)}, u32[]{:S(2)}) copy-start(bf16[2048,1024]{1,0:T(8,128)(2,1)} %proj_ref.1) | copy-start | bytes 12582916
  27.3 1.6 %collective-permute-start.11 = (bf16[64,2048]{1,0:T(8,128)(2,1)S(1)}, bf16[64,2048]{1,0:T(8,128)(2,1)S(1)}, u32[]{:S(2)}, u32[]{:S(2)}) collective-permute-start(bf16[64,2048]{1,0:T(8,128)(2,1)S(1)} %get-tuple-element.33), channel_id=1, source_target_pairs={{0,1},{1,0},{2,3},{3,2},{4,5},{5,4},{6,7},{7,6},{8,9},{9,8},{10,11... | collective-permute-start | bytes 786440 | tf_op jit(solution)/shard_map/ppermute | solution.py:348
  27.9 13.3 %collective-permute-start.10 = (bf16[32,2048]{1,0:T(8,128)(2,1)S(1)}, bf16[32,2048]{1,0:T(8,128)(2,1)S(1)}, u32[]{:S(2)}, u32[]{:S(2)}) collective-permute-start(bf16[32,2048]{1,0:T(8,128)(2,1)S(1)} %get-tuple-element.31), channel_id=1, source_target_pairs={{0,10},{1,9},{2,8},{3,11},{4,14},{5,13},{6,12},{7,15},{8,2},{9,1},... | collective-permute-start | bytes 393224 | tf_op jit(solution)/shard_map/ppermute | solution.py:345
  28.9 12.3 %collective-permute-start.13 = (bf16[32,2048]{1,0:T(8,128)(2,1)S(1)}, bf16[32,2048]{1,0:T(8,128)(2,1)S(1)}, u32[]{:S(2)}, u32[]{:S(2)}) collective-permute-start(bf16[32,2048]{1,0:T(8,128)(2,1)S(1)} %get-tuple-element.41), channel_id=1, source_target_pairs={{0,14},{1,13},{2,12},{3,15},{4,10},{5,9},{6,8},{7,11},{8,6},{9,5},... | collective-permute-start | bytes 393224 | tf_op jit(solution)/shard_map/ppermute | solution.py:345
  32.5 8.7 %collective-permute-start.14 = (bf16[32,2048]{1,0:T(8,128)(2,1)S(1)}, bf16[32,2048]{1,0:T(8,128)(2,1)S(1)}, u32[]{:S(2)}, u32[]{:S(2)}) collective-permute-start(bf16[32,2048]{1,0:T(8,128)(2,1)S(1)} %get-tuple-element.34), channel_id=1, source_target_pairs={{1,3},{3,1},{5,7},{7,5},{9,11},{11,9},{13,15},{15,13},{17,19},{19,... | collective-permute-start | bytes 393224 | tf_op jit(solution)/shard_map/ppermute | solution.py:345
  33.1 10.7 %collective-permute-start.12 = (bf16[32,2048]{1,0:T(8,128)(2,1)S(1)}, bf16[32,2048]{1,0:T(8,128)(2,1)S(1)}, u32[]{:S(2)}, u32[]{:S(2)}) collective-permute-start(bf16[32,2048]{1,0:T(8,128)(2,1)S(1)} %get-tuple-element.40), channel_id=1, source_target_pairs={{0,6},{1,5},{2,4},{3,7},{4,2},{5,1},{6,0},{7,3},{8,14},{9,13},{10,... | collective-permute-start | bytes 393224 | tf_op jit(solution)/shard_map/ppermute | solution.py:345
  43.9 1.3 %collective-permute-start.15 = (bf16[16,2048]{1,0:T(8,128)(2,1)S(1)}, bf16[16,2048]{1,0:T(8,128)(2,1)S(1)}, u32[]{:S(2)}, u32[]{:S(2)}) collective-permute-start(bf16[16,2048]{1,0:T(8,128)(2,1)S(1)} %slice.7), channel_id=1, source_target_pairs={{0,1},{1,0},{2,3},{3,2},{4,5},{5,4},{6,7},{7,6},{8,9},{9,8},{10,11... | collective-permute-start | bytes 196616 | tf_op jit(solution)/shard_map/ppermute | solution.py:348

commit v3 on v2

--- a/solution.py
+++ b/solution.py
@@ -288,12 +288,17 @@
 
 def gather_partners(chips, across):
     others = [m for m in range(1, chips) if m != across]
-    return [others[-2:-1] + others[:-2][0::2], others[-1:] + others[:-2][1::2]]
+    middle = len(others) // 2
+    order = others[middle - 1 : middle + 1] + others[: middle - 1] + others[: middle : -1]
+    return [order[0::2], order[1::2]]
 
 
 def reduce_partners(chips):
     evens = sorted(range(2, chips, 2), key=lambda m: (m != chips // 2, m))
-    return [[m + 1 for m in evens] + [None], evens + [1]]
+    last = chips - 2
+    ones = [m if m == last else m + 1 for m in evens]
+    twos = [m + 1 if m == last else m for m in evens]
+    return [ones + [None], twos + [1]]
 
 
 def in_hbm(x):

time: 47 us -> 47.2 us (level)
  waiting for transfers between devices: 20.1 us -> 21.8 us
  starting transfers between devices: 16.8 us -> 15.3 us
    ppermute x1, waiting for transfers between devices: 5.72 us -> 8.49 us  [both_cores(): return lax.ppermute(x, 'ep', [(i, i ^ 2 * across) for i in range(devices)])]
    ppermute x8, starting transfers between devices: 3.76 us -> 2.16 us  [near(): return lax.ppermute(x, 'ep', [(i, i ^ 1) for i in range(devices)])]
    ppermute x7, waiting for transfers between devices: 11.8 us -> 10.8 us  [far(): return lax.ppermute(x, 'ep', pairs)]
    ppermute x7, starting transfers between devices: 12.5 us -> 13.1 us  [far(): return lax.ppermute(x, 'ep', pairs)]
    ppermute x1, starting transfers between devices: 0.51 us -> 0.01 us  [both_cores(): return lax.ppermute(x, 'ep', [(i, i ^ 2 * across) for i in range(devices)])]
  transfers between devices with their start and end apart: 16 -> 16, of which waited for: 8 -> 7; matrix products, arithmetic and copies ran while one was open for 0% -> 0% of each run, Pallas kernels for 11% -> 11%
where the time goes in v3:
time: 47.2 us; the launch traced here: 47 us
  waiting for transfers between devices  21.8 us (46%)
  starting transfers between devices  15.3 us (32%)
  Pallas kernels  9.24 us (20%)
    ppermute x7, starting transfers between devices, far(): return lax.ppermute(x, 'ep', pairs)  13.1 us
    ppermute x7, waiting for transfers between devices, far(): return lax.ppermute(x, 'ep', pairs)  10.8 us
    pallas_call x10, Pallas kernels, call(): pl.pallas_call(kernel, out_shape=out_shape, in_specs=in_specs or specs, o...  9.24 us
    ppermute x1, waiting for transfers between devices, both_cores(): return lax.ppermute(x, 'ep', [(i, i ^ 2 * across) for i in range(devices)])  8.49 us
    ppermute x8, waiting for transfers between devices, near(): return lax.ppermute(x, 'ep', [(i, i ^ 1) for i in range(devices)])  2.48 us
    ppermute x8, starting transfers between devices, near(): return lax.ppermute(x, 'ep', [(i, i ^ 1) for i in range(devices)])  2.16 us
  transfers between devices with their start and end apart: 16, of which 7 were waited for; matrix products, arithmetic and copies ran while one was open for 0% of the time, Pallas kernels for 11%

profile of v3, /device:TPU:0, one launch (start us, length us, event | category | flops | bytes accessed | tf_op | source)
XLA Modules:
  0.0 47.0 jit_solution(17525417658430807928)
XLA Ops:
  0.0 1.0 %shard_map.137.own_ref = bf16[16,2176]{1,0:T(8,128)(2,1)S(1)} custom-call(bf16[16,2048]{1,0:T(8,128)(2,1)} %rows_ref.1, s32[8,16]{1,0:T(8,128)} %bitcast.11, f32[8,16]{1,0:T(8,128)} %bitcast.12, s32[1,16]{1,0:T(1,128)} %slot_ref.1), custom_call_target="tpu_custom_call" | custom-call | tf_op jit(solution)/shard_map/pallas_call | solution.py:311
  1.0 0.6 %collective-permute-start = (bf16[16,2176]{1,0:T(8,128)(2,1)S(1)}, bf16[16,2176]{1,0:T(8,128)(2,1)S(1)}, u32[]{:S(2)}, u32[]{:S(2)}) collective-permute-start(bf16[16,2176]{1,0:T(8,128)(2,1)S(1)} %shard_map.137.own_ref), channel_id=1, source_target_pairs={{0,1},{1,0},{2,3},{3,2},{4,5},{5,4},{6,7},{7,6},{8,9},{9,8},{10,11... | collective-permute-start | bytes 208904 | tf_op jit(solution)/shard_map/ppermute | solution.py:353
  1.6 0.9 %collective-permute-done.other_ref = bf16[16,2176]{1,0:T(8,128)(2,1)S(1)} collective-permute-done((bf16[16,2176]{1,0:T(8,128)(2,1)S(1)}, bf16[16,2176]{1,0:T(8,128)(2,1)S(1)}, u32[]{:S(2)}, u32[]{:S(2)}) %collective-permute-start) | collective-permute-done | bytes 69664 | tf_op jit(solution)/shard_map/ppermute | solution.py:353
  2.5 2.9 %collective-permute-start.4 = (bf16[32,2176]{1,0:T(8,128)(2,1)S(1)}, bf16[32,2176]{1,0:T(8,128)(2,1)S(1)}, u32[]{:S(2)}, u32[]{:S(2)}) collective-permute-start(bf16[32,2176]{1,0:T(8,128)(2,1)S(1)} %shard_map.138.refs_0_), channel_id=1, source_target_pairs={{0,2},{1,5},{2,0},{3,7},{4,6},{5,1},{6,4},{7,3},{8,10},{9,13},{10,... | collective-permute-start | bytes 417800 | tf_op jit(solution)/shard_map/ppermute | solution.py:350
  5.4 1.5 %collective-permute-start.3 = (bf16[32,2176]{1,0:T(8,128)(2,1)S(1)}, bf16[32,2176]{1,0:T(8,128)(2,1)S(1)}, u32[]{:S(2)}, u32[]{:S(2)}) collective-permute-start(bf16[32,2176]{1,0:T(8,128)(2,1)S(1)} %shard_map.138.refs_0_), channel_id=1, source_target_pairs={{0,6},{1,11},{2,4},{3,9},{4,2},{5,15},{6,0},{7,13},{8,14},{9,3},{1... | collective-permute-start | bytes 417800 | tf_op jit(solution)/shard_map/ppermute | solution.py:350
  6.9 3.4 %collective-permute-start.7 = (bf16[32,2176]{1,0:T(8,128)(2,1)S(1)}, bf16[32,2176]{1,0:T(8,128)(2,1)S(1)}, u32[]{:S(2)}, u32[]{:S(2)}) collective-permute-start(bf16[32,2176]{1,0:T(8,128)(2,1)S(1)} %shard_map.138.refs_0_), channel_id=1, source_target_pairs={{0,14},{1,13},{2,12},{3,15},{4,10},{5,9},{6,8},{7,11},{8,6},{9,5},... | collective-permute-start | bytes 417800 | tf_op jit(solution)/shard_map/ppermute | solution.py:350
  10.4 2.3 %collective-permute-done.3.refs_3_ = bf16[32,2176]{1,0:T(8,128)(2,1)S(1)} collective-permute-done((bf16[32,2176]{1,0:T(8,128)(2,1)S(1)}, bf16[32,2176]{1,0:T(8,128)(2,1)S(1)}, u32[]{:S(2)}, u32[]{:S(2)}) %collective-permute-start.3) | collective-permute-done | bytes 139296 | tf_op jit(solution)/shard_map/ppermute | solution.py:350
  12.7 8.5 %collective-permute-done.1.refs_1_ = bf16[16,2176]{1,0:T(8,128)(2,1)S(1)} collective-permute-done((bf16[16,2176]{1,0:T(8,128)(2,1)S(1)}, bf16[16,2176]{1,0:T(8,128)(2,1)S(1)}, u32[]{:S(2)}, u32[]{:S(2)}) %collective-permute-start.1) | collective-permute-done | bytes 69664 | tf_op jit(solution)/shard_map/ppermute | solution.py:356
  21.2 0.8 %collective-permute-start.2 = (bf16[16,2176]{1,0:T(8,128)(2,1)S(1)}, bf16[16,2176]{1,0:T(8,128)(2,1)S(1)}, u32[]{:S(2)}, u32[]{:S(2)}) collective-permute-start(bf16[16,2176]{1,0:T(8,128)(2,1)S(1)} %collective-permute-done.1.refs_1_), channel_id=1, source_target_pairs={{0,1},{1,0},{2,3},{3,2},{4,5},{5,4},{6,7},{7,6},{8,9},{9,8},{10,11... | collective-permute-start | bytes 208904 | tf_op jit(solution)/shard_map/ppermute | solution.py:353
  22.0 2.4 %shard_map.136 = (bf16[2048,512]{1,0:T(8,128)(2,1)S(1)}, bf16[512,2048]{1,0:T(8,128)(2,1)S(1)}) custom-call(bf16[2048,512]{1,0:T(8,128)(2,1)} %bitcast.9, bf16[512,2048]{1,0:T(8,128)(2,1)} %bitcast.10), custom_call_target="tpu_custom_call" | custom-call | bytes 4194304 | tf_op jit(solution)/shard_map/pallas_call | solution.py:311
  24.8 1.1 %shard_map.139.early_ref = bf16[192,512]{1,0:T(8,128)(2,1)S(1)} custom-call(bf16[2048,512]{1,0:T(8,128)(2,1)S(1)} %bitcast.6, bf16[2048,512]{1,0:T(8,128)(2,1)S(1)} %get-tuple-element.25.wu_ref, bf16[32,2176]{1,0:T(8,128)(2,1)S(1)} %shard_map.138.refs_0_, bf16[16,2176]{1,0:T(8,128)(2,1)S(1)} %collective-permute-done.1.refs_1_, ...), custom_call_target="tpu_custom_call" | custom-call | flops 805306368 | bytes 4194304 | tf_op jit(solution)/shard_map/pallas_call | solution.py:311
  25.9 1.4 %shard_map.140 = (bf16[64,2048]{1,0:T(8,128)(2,1)S(1)}, bf16[224,512]{1,0:T(8,128)(2,1)S(1)}) custom-call(s32[2,256]{1,0:T(2,128)S(1)} %copy-done.6, s32[288,2]{1,0:T(8,128)S(1)} %copy-done.3, bf16[2048,512]{1,0:T(8,128)(2,1)S(1)} %bitcast.7, bf16[2048,512]{1,0:T(8,128)(2,1)S(1)} %get-tuple-element.25.wu_ref, ...), custom_call_target="tpu_custom_call" | custom-call | tf_op jit(solution)/shard_map/pallas_call | solution.py:311
  27.4 0.6 %collective-permute-start.9 = (bf16[64,2048]{1,0:T(8,128)(2,1)S(1)}, bf16[64,2048]{1,0:T(8,128)(2,1)S(1)}, u32[]{:S(2)}, u32[]{:S(2)}) collective-permute-start(bf16[64,2048]{1,0:T(8,128)(2,1)S(1)} %get-tuple-element.30), channel_id=1, source_target_pairs={{0,1},{1,0},{2,3},{3,2},{4,5},{5,4},{6,7},{7,6},{8,9},{9,8},{10,11... | collective-permute-start | bytes 786440 | tf_op jit(solution)/shard_map/ppermute | solution.py:353
  28.0 0.6 %shard_map.141 = (bf16[64,2048]{1,0:T(8,128)(2,1)S(1)}, bf16[64,2048]{1,0:T(8,128)(2,1)S(1)}, bf16[64,2048]{1,0:T(8,128)(2,1)S(1)}, bf16[32,2048]{1,0:T(8,128)(2,1)S(1)}) custom-call(bf16[224,512]{1,0:T(8,128)(2,1)S(1)} %get-tuple-element.27.placed_ref, bf16[512,2048]{1,0:T(8,128)(2,1)S(1)} %get-tuple-element.26.wd_ref), custom_call_target="tpu_custom_call" | custom-call | flops 603979776 | bytes 2097152 | tf_op jit(solution)/shard_map/pallas_call | solution.py:311
  28.7 0.4 collective-permute-done.9.given_ref
  29.2 1.1 %collective-permute-start.10 = (bf16[32,2048]{1,0:T(8,128)(2,1)S(1)}, bf16[32,2048]{1,0:T(8,128)(2,1)S(1)}, u32[]{:S(2)}, u32[]{:S(2)}) collective-permute-start(bf16[32,2048]{1,0:T(8,128)(2,1)S(1)} %get-tuple-element.31), channel_id=1, source_target_pairs={{0,10},{1,9},{2,8},{3,11},{4,14},{5,13},{6,12},{7,15},{8,2},{9,1},... | collective-permute-start | bytes 393224 | tf_op jit(solution)/shard_map/ppermute | solution.py:350
  30.3 2.5 %collective-permute-start.13 = (bf16[32,2048]{1,0:T(8,128)(2,1)S(1)}, bf16[32,2048]{1,0:T(8,128)(2,1)S(1)}, u32[]{:S(2)}, u32[]{:S(2)}) collective-permute-start(bf16[32,2048]{1,0:T(8,128)(2,1)S(1)} %get-tuple-element.41), channel_id=1, source_target_pairs={{0,12},{1,15},{2,14},{3,13},{4,8},{5,11},{6,10},{7,9},{8,4},{9,7},... | collective-permute-start | bytes 393224 | tf_op jit(solution)/shard_map/ppermute | solution.py:350
  32.8 0.7 %collective-permute-start.14 = (bf16[32,2048]{1,0:T(8,128)(2,1)S(1)}, bf16[32,2048]{1,0:T(8,128)(2,1)S(1)}, u32[]{:S(2)}, u32[]{:S(2)}) collective-permute-start(bf16[32,2048]{1,0:T(8,128)(2,1)S(1)} %get-tuple-element.34), channel_id=1, source_target_pairs={{1,3},{3,1},{5,7},{7,5},{9,11},{11,9},{13,15},{15,13},{17,19},{19,... | collective-permute-start | bytes 393224 | tf_op jit(solution)/shard_map/ppermute | solution.py:350
  33.5 1.0 %collective-permute-start.12 = (bf16[32,2048]{1,0:T(8,128)(2,1)S(1)}, bf16[32,2048]{1,0:T(8,128)(2,1)S(1)}, u32[]{:S(2)}, u32[]{:S(2)}) collective-permute-start(bf16[32,2048]{1,0:T(8,128)(2,1)S(1)} %get-tuple-element.40), channel_id=1, source_target_pairs={{0,6},{1,5},{2,4},{3,7},{4,2},{5,1},{6,0},{7,3},{8,14},{9,13},{10,... | collective-permute-start | bytes 393224 | tf_op jit(solution)/shard_map/ppermute | solution.py:350
  34.5 1.0 %shard_map.144 = (bf16[16,2048]{1,0:T(8,128)(2,1)S(1)}, f32[16,4,1024]{2,1,0:T(4,128)S(1)}, f32[16,4,1024]{2,1,0:T(4,128)S(1)}) custom-call(s32[16]{0:T(128)S(1)} %copy-done.7, s32[2,256]{1,0:T(2,128)S(1)} %copy-done.6, bf16[6,16,1024]{2,1,0:T(8,128)(2,1)S(1)} %bitcast.8, f32[4,1024]{1,0:T(4,128)S(1)} %copy-done.5, f32[7,1024]{1,0:T(8,128)S(1)} %copy-done.4, ...), custom_call_target="tpu_custom_call" | custom-call | flops 16777216 | bytes 1048576 | tf_op jit(solution)/shard_map/pallas_call | solution.py:311
  35.6 5.8 %collective-permute-done.10 = bf16[32,2048]{1,0:T(8,128)(2,1)S(1)} collective-permute-done((bf16[32,2048]{1,0:T(8,128)(2,1)S(1)}, bf16[32,2048]{1,0:T(8,128)(2,1)S(1)}, u32[]{:S(2)}, u32[]{:S(2)}) %collective-permute-start.10) | collective-permute-done | bytes 131104 | tf_op jit(solution)/shard_map/ppermute | solution.py:350
  41.4 2.6 %collective-permute-done.12 = bf16[32,2048]{1,0:T(8,128)(2,1)S(1)} collective-permute-done((bf16[32,2048]{1,0:T(8,128)(2,1)S(1)}, bf16[32,2048]{1,0:T(8,128)(2,1)S(1)}, u32[]{:S(2)}, u32[]{:S(2)}) %collective-permute-start.12) | collective-permute-done | bytes 131104 | tf_op jit(solution)/shard_map/ppermute | solution.py:350
  44.3 1.1 %collective-permute-done.15.got_ref = bf16[16,2048]{1,0:T(8,128)(2,1)S(1)} collective-permute-done((bf16[16,2048]{1,0:T(8,128)(2,1)S(1)}, bf16[16,2048]{1,0:T(8,128)(2,1)S(1)}, u32[]{:S(2)}, u32[]{:S(2)}) %collective-permute-start.15) | collective-permute-done | bytes 65568 | tf_op jit(solution)/shard_map/ppermute | solution.py:353
  45.5 1.6 %shard_map.145 = bf16[16,4,1024]{2,1,0:T(4,128)(2,1)} custom-call(f32[32,2048]{1,0:T(8,128)S(1)} %convert_add_fusion.mine_ref, bf16[16,2048]{1,0:T(8,128)(2,1)S(1)} %collective-permute-done.15.got_ref, bf16[16,2048]{1,0:T(8,128)(2,1)S(1)} %get-tuple-element.42.rest_ref, bf16[2048,1024]{1,0:T(8,128)(2,1)S(1)} %copy-done.1, ...), custom_call_target="tpu_custom_call" | custom-call | tf_op jit(solution)/shard_map/pallas_call | solution.py:311
  (36 shorter events, 1.0 us)
Async XLA Ops:
  1.0 1.5 %collective-permute-start = (bf16[16,2176]{1,0:T(8,128)(2,1)S(1)}, bf16[16,2176]{1,0:T(8,128)(2,1)S(1)}, u32[]{:S(2)}, u32[]{:S(2)}) collective-permute-start(bf16[16,2176]{1,0:T(8,128)(2,1)S(1)} %shard_map.137.own_ref), channel_id=1, source_target_pairs={{0,1},{1,0},{2,3},{3,2},{4,5},{5,4},{6,7},{7,6},{8,9},{9,8},{10,11... | collective-permute-start | bytes 208904 | tf_op jit(solution)/shard_map/ppermute | solution.py:353
  2.5 7.9 %collective-permute-start.4 = (bf16[32,2176]{1,0:T(8,128)(2,1)S(1)}, bf16[32,2176]{1,0:T(8,128)(2,1)S(1)}, u32[]{:S(2)}, u32[]{:S(2)}) collective-permute-start(bf16[32,2176]{1,0:T(8,128)(2,1)S(1)} %shard_map.138.refs_0_), channel_id=1, source_target_pairs={{0,2},{1,5},{2,0},{3,7},{4,6},{5,1},{6,4},{7,3},{8,10},{9,13},{10,... | collective-permute-start | bytes 417800 | tf_op jit(solution)/shard_map/ppermute | solution.py:350
  5.4 7.3 %collective-permute-start.3 = (bf16[32,2176]{1,0:T(8,128)(2,1)S(1)}, bf16[32,2176]{1,0:T(8,128)(2,1)S(1)}, u32[]{:S(2)}, u32[]{:S(2)}) collective-permute-start(bf16[32,2176]{1,0:T(8,128)(2,1)S(1)} %shard_map.138.refs_0_), channel_id=1, source_target_pairs={{0,6},{1,11},{2,4},{3,9},{4,2},{5,15},{6,0},{7,13},{8,14},{9,3},{1... | collective-permute-start | bytes 417800 | tf_op jit(solution)/shard_map/ppermute | solution.py:350
  6.9 15.0 %collective-permute-start.7 = (bf16[32,2176]{1,0:T(8,128)(2,1)S(1)}, bf16[32,2176]{1,0:T(8,128)(2,1)S(1)}, u32[]{:S(2)}, u32[]{:S(2)}) collective-permute-start(bf16[32,2176]{1,0:T(8,128)(2,1)S(1)} %shard_map.138.refs_0_), channel_id=1, source_target_pairs={{0,14},{1,13},{2,12},{3,15},{4,10},{5,9},{6,8},{7,11},{8,6},{9,5},... | collective-permute-start | bytes 417800 | tf_op jit(solution)/shard_map/ppermute | solution.py:350
  10.4 10.9 %collective-permute-start.1 = (bf16[16,2176]{1,0:T(8,128)(2,1)S(1)}, bf16[16,2176]{1,0:T(8,128)(2,1)S(1)}, u32[]{:S(2)}, u32[]{:S(2)}) collective-permute-start(bf16[16,2176]{1,0:T(8,128)(2,1)S(1)} %shard_map.137.own_ref), channel_id=1, source_target_pairs={{0,8},{1,9},{2,10},{3,11},{4,12},{5,13},{6,14},{7,15},{8,0},{9,1},... | collective-permute-start | bytes 208904 | tf_op jit(solution)/shard_map/ppermute | solution.py:356
  10.4 14.0 %collective-permute-start.6 = (bf16[32,2176]{1,0:T(8,128)(2,1)S(1)}, bf16[32,2176]{1,0:T(8,128)(2,1)S(1)}, u32[]{:S(2)}, u32[]{:S(2)}) collective-permute-start(bf16[32,2176]{1,0:T(8,128)(2,1)S(1)} %collective-permute-done.4.refs_4_), channel_id=1, source_target_pairs={{0,1},{1,0},{2,3},{3,2},{4,5},{5,4},{6,7},{7,6},{8,9},{9,8},{10,11... | collective-permute-start | bytes 417800 | tf_op jit(solution)/shard_map/ppermute | solution.py:353
  12.7 11.7 %collective-permute-start.5 = (bf16[32,2176]{1,0:T(8,128)(2,1)S(1)}, bf16[32,2176]{1,0:T(8,128)(2,1)S(1)}, u32[]{:S(2)}, u32[]{:S(2)}) collective-permute-start(bf16[32,2176]{1,0:T(8,128)(2,1)S(1)} %collective-permute-done.3.refs_3_), channel_id=1, source_target_pairs={{0,1},{1,0},{2,3},{3,2},{4,5},{5,4},{6,7},{7,6},{8,9},{9,8},{10,11... | collective-permute-start | bytes 417800 | tf_op jit(solution)/shard_map/ppermute | solution.py:353
  21.2 3.2 %collective-permute-start.2 = (bf16[16,2176]{1,0:T(8,128)(2,1)S(1)}, bf16[16,2176]{1,0:T(8,128)(2,1)S(1)}, u32[]{:S(2)}, u32[]{:S(2)}) collective-permute-start(bf16[16,2176]{1,0:T(8,128)(2,1)S(1)} %collective-permute-done.1.refs_1_), channel_id=1, source_target_pairs={{0,1},{1,0},{2,3},{3,2},{4,5},{5,4},{6,7},{7,6},{8,9},{9,8},{10,11... | collective-permute-start | bytes 208904 | tf_op jit(solution)/shard_map/ppermute | solution.py:353
  22.0 3.9 %collective-permute-start.8 = (bf16[32,2176]{1,0:T(8,128)(2,1)S(1)}, bf16[32,2176]{1,0:T(8,128)(2,1)S(1)}, u32[]{:S(2)}, u32[]{:S(2)}) collective-permute-start(bf16[32,2176]{1,0:T(8,128)(2,1)S(1)} %collective-permute-done.7.refs_0_.refs_7_), channel_id=1, source_target_pairs={{0,1},{1,0},{2,3},{3,2},{4,5},{5,4},{6,7},{7,6},{8,9},{9,8},{10,11... | collective-permute-start | bytes 417800 | tf_op jit(solution)/shard_map/ppermute | solution.py:353
  22.0 2.9 %copy-start = (bf16[1,2048,512]{2,1,0:T(8,128)(2,1)S(1)}, bf16[1,2048,512]{2,1,0:T(8,128)(2,1)}, u32[]{:S(2)}) copy-start(bf16[1,2048,512]{2,1,0:T(8,128)(2,1)} %param.17) | copy-start | bytes 6291460
  24.8 1.1 %copy-start.3 = (s32[288,2]{1,0:T(8,128)S(1)}, s32[288,2]{1,0:T(8,128)}, u32[]{:S(2)}) copy-start(s32[288,2]{1,0:T(8,128)} %constant.5.clone.target_ref) | copy-start | bytes 6916
  24.8 1.1 %copy-start.6 = (s32[2,256]{1,0:T(2,128)S(1)}, s32[2,256]{1,0:T(2,128)}, u32[]{:S(2)}) copy-start(s32[2,256]{1,0:T(2,128)} %constant.4.clone.table_ref) | copy-start | bytes 6148
  27.4 7.2 %copy-start.2 = (bf16[16,6,1024]{2,0,1:T(8,128)(2,1)S(1)}, bf16[16,6,1024]{2,0,1:T(8,128)(2,1)}, u32[]{:S(2)}) copy-start(bf16[16,6,1024]{2,0,1:T(8,128)(2,1)} %param.23) | copy-start | bytes 589828
  27.4 7.2 %copy-start.4 = (f32[7,1024]{1,0:T(8,128)S(1)}, f32[7,1024]{1,0:T(8,128)}, u32[]{:S(2)}) copy-start(f32[7,1024]{1,0:T(8,128)} %conv_ref.1) | copy-start | bytes 86020
  27.4 7.2 %copy-start.5 = (f32[4,1024]{1,0:T(4,128)S(1)}, f32[4,1024]{1,0:T(4,128)}, u32[]{:S(2)}) copy-start(f32[4,1024]{1,0:T(4,128)} %offset_ref.1) | copy-start | bytes 49156
  27.4 7.1 %copy-start.7 = (s32[16]{0:T(128)S(1)}, s32[16]{0:T(128)}, u32[]{:S(2)}) copy-start(s32[16]{0:T(128)} %count_ref.1) | copy-start | bytes 196
  27.4 1.7 %collective-permute-start.9 = (bf16[64,2048]{1,0:T(8,128)(2,1)S(1)}, bf16[64,2048]{1,0:T(8,128)(2,1)S(1)}, u32[]{:S(2)}, u32[]{:S(2)}) collective-permute-start(bf16[64,2048]{1,0:T(8,128)(2,1)S(1)} %get-tuple-element.30), channel_id=1, source_target_pairs={{0,1},{1,0},{2,3},{3,2},{4,5},{5,4},{6,7},{7,6},{8,9},{9,8},{10,11... | collective-permute-start | bytes 786440 | tf_op jit(solution)/shard_map/ppermute | solution.py:353
  28.0 17.5 %copy-start.1 = (bf16[2048,1024]{1,0:T(8,128)(2,1)S(1)}, bf16[2048,1024]{1,0:T(8,128)(2,1)}, u32[]{:S(2)}) copy-start(bf16[2048,1024]{1,0:T(8,128)(2,1)} %proj_ref.1) | copy-start | bytes 12582916
  28.6 1.6 %collective-permute-start.11 = (bf16[64,2048]{1,0:T(8,128)(2,1)S(1)}, bf16[64,2048]{1,0:T(8,128)(2,1)S(1)}, u32[]{:S(2)}, u32[]{:S(2)}) collective-permute-start(bf16[64,2048]{1,0:T(8,128)(2,1)S(1)} %get-tuple-element.33), channel_id=1, source_target_pairs={{0,1},{1,0},{2,3},{3,2},{4,5},{5,4},{6,7},{7,6},{8,9},{9,8},{10,11... | collective-permute-start | bytes 786440 | tf_op jit(solution)/shard_map/ppermute | solution.py:353
  29.2 12.2 %collective-permute-start.10 = (bf16[32,2048]{1,0:T(8,128)(2,1)S(1)}, bf16[32,2048]{1,0:T(8,128)(2,1)S(1)}, u32[]{:S(2)}, u32[]{:S(2)}) collective-permute-start(bf16[32,2048]{1,0:T(8,128)(2,1)S(1)} %get-tuple-element.31), channel_id=1, source_target_pairs={{0,10},{1,9},{2,8},{3,11},{4,14},{5,13},{6,12},{7,15},{8,2},{9,1},... | collective-permute-start | bytes 393224 | tf_op jit(solution)/shard_map/ppermute | solution.py:350
  30.3 11.1 %collective-permute-start.13 = (bf16[32,2048]{1,0:T(8,128)(2,1)S(1)}, bf16[32,2048]{1,0:T(8,128)(2,1)S(1)}, u32[]{:S(2)}, u32[]{:S(2)}) collective-permute-start(bf16[32,2048]{1,0:T(8,128)(2,1)S(1)} %get-tuple-element.41), channel_id=1, source_target_pairs={{0,12},{1,15},{2,14},{3,13},{4,8},{5,11},{6,10},{7,9},{8,4},{9,7},... | collective-permute-start | bytes 393224 | tf_op jit(solution)/shard_map/ppermute | solution.py:350
  32.8 8.6 %collective-permute-start.14 = (bf16[32,2048]{1,0:T(8,128)(2,1)S(1)}, bf16[32,2048]{1,0:T(8,128)(2,1)S(1)}, u32[]{:S(2)}, u32[]{:S(2)}) collective-permute-start(bf16[32,2048]{1,0:T(8,128)(2,1)S(1)} %get-tuple-element.34), channel_id=1, source_target_pairs={{1,3},{3,1},{5,7},{7,5},{9,11},{11,9},{13,15},{15,13},{17,19},{19,... | collective-permute-start | bytes 393224 | tf_op jit(solution)/shard_map/ppermute | solution.py:350
  33.5 10.5 %collective-permute-start.12 = (bf16[32,2048]{1,0:T(8,128)(2,1)S(1)}, bf16[32,2048]{1,0:T(8,128)(2,1)S(1)}, u32[]{:S(2)}, u32[]{:S(2)}) collective-permute-start(bf16[32,2048]{1,0:T(8,128)(2,1)S(1)} %get-tuple-element.40), channel_id=1, source_target_pairs={{0,6},{1,5},{2,4},{3,7},{4,2},{5,1},{6,0},{7,3},{8,14},{9,13},{10,... | collective-permute-start | bytes 393224 | tf_op jit(solution)/shard_map/ppermute | solution.py:350
  44.1 1.3 %collective-permute-start.15 = (bf16[16,2048]{1,0:T(8,128)(2,1)S(1)}, bf16[16,2048]{1,0:T(8,128)(2,1)S(1)}, u32[]{:S(2)}, u32[]{:S(2)}) collective-permute-start(bf16[16,2048]{1,0:T(8,128)(2,1)S(1)} %slice.7), channel_id=1, source_target_pairs={{0,1},{1,0},{2,3},{3,2},{4,5},{5,4},{6,7},{7,6},{8,9},{9,8},{10,11... | collective-permute-start | bytes 196616 | tf_op jit(solution)/shard_map/ppermute | solution.py:353

commit v4 on v3

--- a/solution.py
+++ b/solution.py
@@ -368,11 +368,11 @@
         blocks += side(ours[:-1], 0) + side(theirs[:-1], 1)
         return spread(blocks + side(ours[-1:], 0) + side(theirs[-1:], 1))
 
-    half = slots // 2
     table = np.stack([arriving(c) for c in range(2)])
     keep_to = np.stack([spread(side(back[c], 0) + [0, 1]) for c in range(2)], axis=1)
     give_to = np.stack([spread(side(back[1 - c], 1)) for c in range(2)], axis=1)
-    cut = 2 * rows * half
+    cut = 2 * rows
+    left = cut * (slots - 1)
     target = np.concatenate([give_to, keep_to])
 
     own = call(
@@ -425,7 +425,7 @@
     given = [near(give)]
     give, *keep, here = call(
         rest_kernel,
-        [bf16((cut, features))] * 3 + [bf16((2 * rows, features))],
+        [bf16((n, features)) for n in (left, cut, left, cut)],
         [placed, w_down_here],
         megabytes=6,
         cost=pl.CostEstimate(
@@ -437,7 +437,9 @@
     given.append(near(give))
     chip_sum = []
     for k in range(2):
-        chip_sum += call(sum_kernel, [bf16((2 * rows, features))] * half, [keep[k], given[k]])
+        chip_sum += call(
+            sum_kernel, [bf16((cut, features))] * (1, slots - 1)[k], [keep[k], given[k]]
+        )
     arrived = [far(chip_sum[j], back, j) for j in range(slots)]
     context, _ = lax.optimization_barrier((left_context.transpose(1, 0, 2), chip_sum[-1]))
     frames = jax.ShapeDtypeStruct((rows, horizon, talker_width), jnp.float32)

time: 47.2 us -> 46.3 us (0.981)
  waiting for transfers between devices: 21.8 us -> 19.9 us
  starting transfers between devices: 15.3 us -> 16 us
    ppermute x7, waiting for transfers between devices: 10.8 us -> 7.77 us  [far(): return lax.ppermute(x, 'ep', pairs)]
    ppermute x8, waiting for transfers between devices: 2.48 us -> 3.62 us  [near(): return lax.ppermute(x, 'ep', [(i, i ^ 1) for i in range(devices)])]
    ppermute x7, starting transfers between devices: 13.1 us -> 13.9 us  [far(): return lax.ppermute(x, 'ep', pairs)]
  transfers between devices with their start and end apart: 16 -> 16, of which waited for: 7 -> 7; matrix products, arithmetic and copies ran while one was open for 0% -> 0% of each run, Pallas kernels for 11% -> 10%
where the time goes in v4:
time: 46.3 us; the launch traced here: 45.9 us
  waiting for transfers between devices  19.9 us (43%)
  starting transfers between devices  16 us (35%)
  Pallas kernels  9.29 us (20%)
  local copies, waits for them, and re-layouts  0.47 us (1%)
    ppermute x7, starting transfers between devices, far(): return lax.ppermute(x, 'ep', pairs)  13.9 us
    pallas_call x10, Pallas kernels, call(): pl.pallas_call(kernel, out_shape=out_shape, in_specs=in_specs or specs, o...  9.29 us
    ppermute x1, waiting for transfers between devices, both_cores(): return lax.ppermute(x, 'ep', [(i, i ^ 2 * across) for i in range(devices)])  8.49 us
    ppermute x7, waiting for transfers between devices, far(): return lax.ppermute(x, 'ep', pairs)  7.77 us
    ppermute x8, waiting for transfers between devices, near(): return lax.ppermute(x, 'ep', [(i, i ^ 1) for i in range(devices)])  3.62 us
    ppermute x8, starting transfers between devices, near(): return lax.ppermute(x, 'ep', [(i, i ^ 1) for i in range(devices)])  2.03 us
  transfers between devices with their start and end apart: 16, of which 7 were waited for; matrix products, arithmetic and copies ran while one was open for 0% of the time, Pallas kernels for 10%

profile of v4, /device:TPU:0, one launch (start us, length us, event | category | flops | bytes accessed | tf_op | source)
XLA Modules:
  0.0 45.9 jit_solution(5974143167628480899)
XLA Ops:
  0.0 1.0 %shard_map.137.own_ref = bf16[16,2176]{1,0:T(8,128)(2,1)S(1)} custom-call(bf16[16,2048]{1,0:T(8,128)(2,1)} %rows_ref.1, s32[8,16]{1,0:T(8,128)} %bitcast.11, f32[8,16]{1,0:T(8,128)} %bitcast.12, s32[1,16]{1,0:T(1,128)} %slot_ref.1), custom_call_target="tpu_custom_call" | custom-call | tf_op jit(solution)/shard_map/pallas_call | solution.py:311
  1.0 0.6 %collective-permute-start = (bf16[16,2176]{1,0:T(8,128)(2,1)S(1)}, bf16[16,2176]{1,0:T(8,128)(2,1)S(1)}, u32[]{:S(2)}, u32[]{:S(2)}) collective-permute-start(bf16[16,2176]{1,0:T(8,128)(2,1)S(1)} %shard_map.137.own_ref), channel_id=1, source_target_pairs={{0,1},{1,0},{2,3},{3,2},{4,5},{5,4},{6,7},{7,6},{8,9},{9,8},{10,11... | collective-permute-start | bytes 208904 | tf_op jit(solution)/shard_map/ppermute | solution.py:353
  1.6 0.9 %collective-permute-done.other_ref = bf16[16,2176]{1,0:T(8,128)(2,1)S(1)} collective-permute-done((bf16[16,2176]{1,0:T(8,128)(2,1)S(1)}, bf16[16,2176]{1,0:T(8,128)(2,1)S(1)}, u32[]{:S(2)}, u32[]{:S(2)}) %collective-permute-start) | collective-permute-done | bytes 69664 | tf_op jit(solution)/shard_map/ppermute | solution.py:353
  2.5 2.9 %collective-permute-start.4 = (bf16[32,2176]{1,0:T(8,128)(2,1)S(1)}, bf16[32,2176]{1,0:T(8,128)(2,1)S(1)}, u32[]{:S(2)}, u32[]{:S(2)}) collective-permute-start(bf16[32,2176]{1,0:T(8,128)(2,1)S(1)} %shard_map.138.refs_0_), channel_id=1, source_target_pairs={{0,2},{1,5},{2,0},{3,7},{4,6},{5,1},{6,4},{7,3},{8,10},{9,13},{10,... | collective-permute-start | bytes 417800 | tf_op jit(solution)/shard_map/ppermute | solution.py:350
  5.4 1.5 %collective-permute-start.3 = (bf16[32,2176]{1,0:T(8,128)(2,1)S(1)}, bf16[32,2176]{1,0:T(8,128)(2,1)S(1)}, u32[]{:S(2)}, u32[]{:S(2)}) collective-permute-start(bf16[32,2176]{1,0:T(8,128)(2,1)S(1)} %shard_map.138.refs_0_), channel_id=1, source_target_pairs={{0,6},{1,11},{2,4},{3,9},{4,2},{5,15},{6,0},{7,13},{8,14},{9,3},{1... | collective-permute-start | bytes 417800 | tf_op jit(solution)/shard_map/ppermute | solution.py:350
  6.9 3.4 %collective-permute-start.7 = (bf16[32,2176]{1,0:T(8,128)(2,1)S(1)}, bf16[32,2176]{1,0:T(8,128)(2,1)S(1)}, u32[]{:S(2)}, u32[]{:S(2)}) collective-permute-start(bf16[32,2176]{1,0:T(8,128)(2,1)S(1)} %shard_map.138.refs_0_), channel_id=1, source_target_pairs={{0,14},{1,13},{2,12},{3,15},{4,10},{5,9},{6,8},{7,11},{8,6},{9,5},... | collective-permute-start | bytes 417800 | tf_op jit(solution)/shard_map/ppermute | solution.py:350
  10.4 2.3 %collective-permute-done.3.refs_3_ = bf16[32,2176]{1,0:T(8,128)(2,1)S(1)} collective-permute-done((bf16[32,2176]{1,0:T(8,128)(2,1)S(1)}, bf16[32,2176]{1,0:T(8,128)(2,1)S(1)}, u32[]{:S(2)}, u32[]{:S(2)}) %collective-permute-start.3) | collective-permute-done | bytes 139296 | tf_op jit(solution)/shard_map/ppermute | solution.py:350
  12.7 8.5 %collective-permute-done.1.refs_1_ = bf16[16,2176]{1,0:T(8,128)(2,1)S(1)} collective-permute-done((bf16[16,2176]{1,0:T(8,128)(2,1)S(1)}, bf16[16,2176]{1,0:T(8,128)(2,1)S(1)}, u32[]{:S(2)}, u32[]{:S(2)}) %collective-permute-start.1) | collective-permute-done | bytes 69664 | tf_op jit(solution)/shard_map/ppermute | solution.py:356
  21.2 0.8 %collective-permute-start.2 = (bf16[16,2176]{1,0:T(8,128)(2,1)S(1)}, bf16[16,2176]{1,0:T(8,128)(2,1)S(1)}, u32[]{:S(2)}, u32[]{:S(2)}) collective-permute-start(bf16[16,2176]{1,0:T(8,128)(2,1)S(1)} %collective-permute-done.1.refs_1_), channel_id=1, source_target_pairs={{0,1},{1,0},{2,3},{3,2},{4,5},{5,4},{6,7},{7,6},{8,9},{9,8},{10,11... | collective-permute-start | bytes 208904 | tf_op jit(solution)/shard_map/ppermute | solution.py:353
  22.0 2.4 %shard_map.136 = (bf16[2048,512]{1,0:T(8,128)(2,1)S(1)}, bf16[512,2048]{1,0:T(8,128)(2,1)S(1)}) custom-call(bf16[2048,512]{1,0:T(8,128)(2,1)} %bitcast.9, bf16[512,2048]{1,0:T(8,128)(2,1)} %bitcast.10), custom_call_target="tpu_custom_call" | custom-call | bytes 4194304 | tf_op jit(solution)/shard_map/pallas_call | solution.py:311
  24.8 1.1 %shard_map.139.early_ref = bf16[192,512]{1,0:T(8,128)(2,1)S(1)} custom-call(bf16[2048,512]{1,0:T(8,128)(2,1)S(1)} %bitcast.6, bf16[2048,512]{1,0:T(8,128)(2,1)S(1)} %get-tuple-element.24.wu_ref, bf16[32,2176]{1,0:T(8,128)(2,1)S(1)} %shard_map.138.refs_0_, bf16[16,2176]{1,0:T(8,128)(2,1)S(1)} %collective-permute-done.1.refs_1_, ...), custom_call_target="tpu_custom_call" | custom-call | flops 805306368 | bytes 4194304 | tf_op jit(solution)/shard_map/pallas_call | solution.py:311
  25.9 1.4 %shard_map.140 = (bf16[32,2048]{1,0:T(8,128)(2,1)S(1)}, bf16[256,512]{1,0:T(8,128)(2,1)S(1)}) custom-call(s32[2,256]{1,0:T(2,128)S(1)} %copy-done.6, s32[288,2]{1,0:T(8,128)S(1)} %copy-done.3, bf16[2048,512]{1,0:T(8,128)(2,1)S(1)} %bitcast.7, bf16[2048,512]{1,0:T(8,128)(2,1)S(1)} %get-tuple-element.24.wu_ref, ...), custom_call_target="tpu_custom_call" | custom-call | tf_op jit(solution)/shard_map/pallas_call | solution.py:311
  27.4 0.7 %shard_map.141 = (bf16[96,2048]{1,0:T(8,128)(2,1)S(1)}, bf16[32,2048]{1,0:T(8,128)(2,1)S(1)}, bf16[96,2048]{1,0:T(8,128)(2,1)S(1)}, bf16[32,2048]{1,0:T(8,128)(2,1)S(1)}) custom-call(bf16[256,512]{1,0:T(8,128)(2,1)S(1)} %get-tuple-element.26.placed_ref, bf16[512,2048]{1,0:T(8,128)(2,1)S(1)} %get-tuple-element.25.wd_ref), custom_call_target="tpu_custom_call" | custom-call | flops 603979776 | bytes 2097152 | tf_op jit(solution)/shard_map/pallas_call | solution.py:311
  28.1 0.6 %collective-permute-start.11 = (bf16[96,2048]{1,0:T(8,128)(2,1)S(1)}, bf16[96,2048]{1,0:T(8,128)(2,1)S(1)}, u32[]{:S(2)}, u32[]{:S(2)}) collective-permute-start(bf16[96,2048]{1,0:T(8,128)(2,1)S(1)} %get-tuple-element.31), channel_id=1, source_target_pairs={{0,1},{1,0},{2,3},{3,2},{4,5},{5,4},{6,7},{7,6},{8,9},{9,8},{10,11... | collective-permute-start | bytes 1179656 | tf_op jit(solution)/shard_map/ppermute | solution.py:353
  28.8 1.5 %collective-permute-done.9.given_ref = bf16[32,2048]{1,0:T(8,128)(2,1)S(1)} collective-permute-done((bf16[32,2048]{1,0:T(8,128)(2,1)S(1)}, bf16[32,2048]{1,0:T(8,128)(2,1)S(1)}, u32[]{:S(2)}, u32[]{:S(2)}) %collective-permute-start.9) | collective-permute-done | bytes 131104 | tf_op jit(solution)/shard_map/ppermute | solution.py:353
  30.3 1.1 %collective-permute-start.10 = (bf16[32,2048]{1,0:T(8,128)(2,1)S(1)}, bf16[32,2048]{1,0:T(8,128)(2,1)S(1)}, u32[]{:S(2)}, u32[]{:S(2)}) collective-permute-start(bf16[32,2048]{1,0:T(8,128)(2,1)S(1)} %shard_map.142), channel_id=1, source_target_pairs={{0,10},{1,9},{2,8},{3,11},{4,14},{5,13},{6,12},{7,15},{8,2},{9,1},... | collective-permute-start | bytes 393224 | tf_op jit(solution)/shard_map/ppermute | solution.py:350
  31.4 3.3 %collective-permute-start.12 = (bf16[32,2048]{1,0:T(8,128)(2,1)S(1)}, bf16[32,2048]{1,0:T(8,128)(2,1)S(1)}, u32[]{:S(2)}, u32[]{:S(2)}) collective-permute-start(bf16[32,2048]{1,0:T(8,128)(2,1)S(1)} %get-tuple-element.38), channel_id=1, source_target_pairs={{0,6},{1,5},{2,4},{3,7},{4,2},{5,1},{6,0},{7,3},{8,14},{9,13},{10,... | collective-permute-start | bytes 393224 | tf_op jit(solution)/shard_map/ppermute | solution.py:350
  34.7 1.1 %collective-permute-start.13 = (bf16[32,2048]{1,0:T(8,128)(2,1)S(1)}, bf16[32,2048]{1,0:T(8,128)(2,1)S(1)}, u32[]{:S(2)}, u32[]{:S(2)}) collective-permute-start(bf16[32,2048]{1,0:T(8,128)(2,1)S(1)} %get-tuple-element.39), channel_id=1, source_target_pairs={{0,12},{1,15},{2,14},{3,13},{4,8},{5,11},{6,10},{7,9},{8,4},{9,7},... | collective-permute-start | bytes 393224 | tf_op jit(solution)/shard_map/ppermute | solution.py:350
  35.8 0.7 %collective-permute-start.14 = (bf16[32,2048]{1,0:T(8,128)(2,1)S(1)}, bf16[32,2048]{1,0:T(8,128)(2,1)S(1)}, u32[]{:S(2)}, u32[]{:S(2)}) collective-permute-start(bf16[32,2048]{1,0:T(8,128)(2,1)S(1)} %get-tuple-element.32), channel_id=1, source_target_pairs={{1,3},{3,1},{5,7},{7,5},{9,11},{11,9},{13,15},{15,13},{17,19},{19,... | collective-permute-start | bytes 393224 | tf_op jit(solution)/shard_map/ppermute | solution.py:350
  36.5 1.0 %shard_map.144 = (bf16[16,2048]{1,0:T(8,128)(2,1)S(1)}, f32[16,4,1024]{2,1,0:T(4,128)S(1)}, f32[16,4,1024]{2,1,0:T(4,128)S(1)}) custom-call(s32[16]{0:T(128)S(1)} %copy-done.7, s32[2,256]{1,0:T(2,128)S(1)} %copy-done.6, bf16[6,16,1024]{2,1,0:T(8,128)(2,1)S(1)} %bitcast.8, f32[4,1024]{1,0:T(4,128)S(1)} %copy-done.5, f32[7,1024]{1,0:T(8,128)S(1)} %copy-done.4, ...), custom_call_target="tpu_custom_call" | custom-call | flops 16777216 | bytes 1048576 | tf_op jit(solution)/shard_map/pallas_call | solution.py:311
  37.5 5.0 %collective-permute-done.10 = bf16[32,2048]{1,0:T(8,128)(2,1)S(1)} collective-permute-done((bf16[32,2048]{1,0:T(8,128)(2,1)S(1)}, bf16[32,2048]{1,0:T(8,128)(2,1)S(1)}, u32[]{:S(2)}, u32[]{:S(2)}) %collective-permute-start.10) | collective-permute-done | bytes 131104 | tf_op jit(solution)/shard_map/ppermute | solution.py:350
  42.5 0.4 collective-permute-done.12
  43.1 1.2 %collective-permute-done.15.got_ref = bf16[16,2048]{1,0:T(8,128)(2,1)S(1)} collective-permute-done((bf16[16,2048]{1,0:T(8,128)(2,1)S(1)}, bf16[16,2048]{1,0:T(8,128)(2,1)S(1)}, u32[]{:S(2)}, u32[]{:S(2)}) %collective-permute-start.15) | collective-permute-done | bytes 65568 | tf_op jit(solution)/shard_map/ppermute | solution.py:353
  44.4 1.6 %shard_map.145 = bf16[16,4,1024]{2,1,0:T(4,128)(2,1)} custom-call(f32[32,2048]{1,0:T(8,128)S(1)} %convert_add_fusion.mine_ref, bf16[16,2048]{1,0:T(8,128)(2,1)S(1)} %collective-permute-done.15.got_ref, bf16[16,2048]{1,0:T(8,128)(2,1)S(1)} %get-tuple-element.40.rest_ref, bf16[2048,1024]{1,0:T(8,128)(2,1)S(1)} %copy-done.1, ...), custom_call_target="tpu_custom_call" | custom-call | tf_op jit(solution)/shard_map/pallas_call | solution.py:311
  (36 shorter events, 0.9 us)
Async XLA Ops:
  1.0 1.5 %collective-permute-start = (bf16[16,2176]{1,0:T(8,128)(2,1)S(1)}, bf16[16,2176]{1,0:T(8,128)(2,1)S(1)}, u32[]{:S(2)}, u32[]{:S(2)}) collective-permute-start(bf16[16,2176]{1,0:T(8,128)(2,1)S(1)} %shard_map.137.own_ref), channel_id=1, source_target_pairs={{0,1},{1,0},{2,3},{3,2},{4,5},{5,4},{6,7},{7,6},{8,9},{9,8},{10,11... | collective-permute-start | bytes 208904 | tf_op jit(solution)/shard_map/ppermute | solution.py:353
  2.5 7.9 %collective-permute-start.4 = (bf16[32,2176]{1,0:T(8,128)(2,1)S(1)}, bf16[32,2176]{1,0:T(8,128)(2,1)S(1)}, u32[]{:S(2)}, u32[]{:S(2)}) collective-permute-start(bf16[32,2176]{1,0:T(8,128)(2,1)S(1)} %shard_map.138.refs_0_), channel_id=1, source_target_pairs={{0,2},{1,5},{2,0},{3,7},{4,6},{5,1},{6,4},{7,3},{8,10},{9,13},{10,... | collective-permute-start | bytes 417800 | tf_op jit(solution)/shard_map/ppermute | solution.py:350
  5.4 7.3 %collective-permute-start.3 = (bf16[32,2176]{1,0:T(8,128)(2,1)S(1)}, bf16[32,2176]{1,0:T(8,128)(2,1)S(1)}, u32[]{:S(2)}, u32[]{:S(2)}) collective-permute-start(bf16[32,2176]{1,0:T(8,128)(2,1)S(1)} %shard_map.138.refs_0_), channel_id=1, source_target_pairs={{0,6},{1,11},{2,4},{3,9},{4,2},{5,15},{6,0},{7,13},{8,14},{9,3},{1... | collective-permute-start | bytes 417800 | tf_op jit(solution)/shard_map/ppermute | solution.py:350
  6.9 15.0 %collective-permute-start.7 = (bf16[32,2176]{1,0:T(8,128)(2,1)S(1)}, bf16[32,2176]{1,0:T(8,128)(2,1)S(1)}, u32[]{:S(2)}, u32[]{:S(2)}) collective-permute-start(bf16[32,2176]{1,0:T(8,128)(2,1)S(1)} %shard_map.138.refs_0_), channel_id=1, source_target_pairs={{0,14},{1,13},{2,12},{3,15},{4,10},{5,9},{6,8},{7,11},{8,6},{9,5},... | collective-permute-start | bytes 417800 | tf_op jit(solution)/shard_map/ppermute | solution.py:350
  10.4 10.9 %collective-permute-start.1 = (bf16[16,2176]{1,0:T(8,128)(2,1)S(1)}, bf16[16,2176]{1,0:T(8,128)(2,1)S(1)}, u32[]{:S(2)}, u32[]{:S(2)}) collective-permute-start(bf16[16,2176]{1,0:T(8,128)(2,1)S(1)} %shard_map.137.own_ref), channel_id=1, source_target_pairs={{0,8},{1,9},{2,10},{3,11},{4,12},{5,13},{6,14},{7,15},{8,0},{9,1},... | collective-permute-start | bytes 208904 | tf_op jit(solution)/shard_map/ppermute | solution.py:356
  10.4 14.0 %collective-permute-start.6 = (bf16[32,2176]{1,0:T(8,128)(2,1)S(1)}, bf16[32,2176]{1,0:T(8,128)(2,1)S(1)}, u32[]{:S(2)}, u32[]{:S(2)}) collective-permute-start(bf16[32,2176]{1,0:T(8,128)(2,1)S(1)} %collective-permute-done.4.refs_4_), channel_id=1, source_target_pairs={{0,1},{1,0},{2,3},{3,2},{4,5},{5,4},{6,7},{7,6},{8,9},{9,8},{10,11... | collective-permute-start | bytes 417800 | tf_op jit(solution)/shard_map/ppermute | solution.py:353
  12.7 11.7 %collective-permute-start.5 = (bf16[32,2176]{1,0:T(8,128)(2,1)S(1)}, bf16[32,2176]{1,0:T(8,128)(2,1)S(1)}, u32[]{:S(2)}, u32[]{:S(2)}) collective-permute-start(bf16[32,2176]{1,0:T(8,128)(2,1)S(1)} %collective-permute-done.3.refs_3_), channel_id=1, source_target_pairs={{0,1},{1,0},{2,3},{3,2},{4,5},{5,4},{6,7},{7,6},{8,9},{9,8},{10,11... | collective-permute-start | bytes 417800 | tf_op jit(solution)/shard_map/ppermute | solution.py:353
  21.2 3.2 %collective-permute-start.2 = (bf16[16,2176]{1,0:T(8,128)(2,1)S(1)}, bf16[16,2176]{1,0:T(8,128)(2,1)S(1)}, u32[]{:S(2)}, u32[]{:S(2)}) collective-permute-start(bf16[16,2176]{1,0:T(8,128)(2,1)S(1)} %collective-permute-done.1.refs_1_), channel_id=1, source_target_pairs={{0,1},{1,0},{2,3},{3,2},{4,5},{5,4},{6,7},{7,6},{8,9},{9,8},{10,11... | collective-permute-start | bytes 208904 | tf_op jit(solution)/shard_map/ppermute | solution.py:353
  22.0 3.9 %collective-permute-start.8 = (bf16[32,2176]{1,0:T(8,128)(2,1)S(1)}, bf16[32,2176]{1,0:T(8,128)(2,1)S(1)}, u32[]{:S(2)}, u32[]{:S(2)}) collective-permute-start(bf16[32,2176]{1,0:T(8,128)(2,1)S(1)} %collective-permute-done.7.refs_0_.refs_7_), channel_id=1, source_target_pairs={{0,1},{1,0},{2,3},{3,2},{4,5},{5,4},{6,7},{7,6},{8,9},{9,8},{10,11... | collective-permute-start | bytes 417800 | tf_op jit(solution)/shard_map/ppermute | solution.py:353
  22.0 2.9 %copy-start = (bf16[1,2048,512]{2,1,0:T(8,128)(2,1)S(1)}, bf16[1,2048,512]{2,1,0:T(8,128)(2,1)}, u32[]{:S(2)}) copy-start(bf16[1,2048,512]{2,1,0:T(8,128)(2,1)} %param.17) | copy-start | bytes 6291460
  24.8 1.1 %copy-start.3 = (s32[288,2]{1,0:T(8,128)S(1)}, s32[288,2]{1,0:T(8,128)}, u32[]{:S(2)}) copy-start(s32[288,2]{1,0:T(8,128)} %constant.5.clone.target_ref) | copy-start | bytes 6916
  24.8 1.1 %copy-start.6 = (s32[2,256]{1,0:T(2,128)S(1)}, s32[2,256]{1,0:T(2,128)}, u32[]{:S(2)}) copy-start(s32[2,256]{1,0:T(2,128)} %constant.4.clone.table_ref) | copy-start | bytes 6148
  27.3 9.1 %copy-start.2 = (bf16[16,6,1024]{2,0,1:T(8,128)(2,1)S(1)}, bf16[16,6,1024]{2,0,1:T(8,128)(2,1)}, u32[]{:S(2)}) copy-start(bf16[16,6,1024]{2,0,1:T(8,128)(2,1)} %param.23) | copy-start | bytes 589828
  27.4 9.1 %copy-start.4 = (f32[7,1024]{1,0:T(8,128)S(1)}, f32[7,1024]{1,0:T(8,128)}, u32[]{:S(2)}) copy-start(f32[7,1024]{1,0:T(8,128)} %conv_ref.1) | copy-start | bytes 86020
  27.4 9.1 %copy-start.5 = (f32[4,1024]{1,0:T(4,128)S(1)}, f32[4,1024]{1,0:T(4,128)}, u32[]{:S(2)}) copy-start(f32[4,1024]{1,0:T(4,128)} %offset_ref.1) | copy-start | bytes 49156
  27.4 9.1 %copy-start.7 = (s32[16]{0:T(128)S(1)}, s32[16]{0:T(128)}, u32[]{:S(2)}) copy-start(s32[16]{0:T(128)} %count_ref.1) | copy-start | bytes 196
  27.4 17.0 %copy-start.1 = (bf16[2048,1024]{1,0:T(8,128)(2,1)S(1)}, bf16[2048,1024]{1,0:T(8,128)(2,1)}, u32[]{:S(2)}) copy-start(bf16[2048,1024]{1,0:T(8,128)(2,1)} %proj_ref.1) | copy-start | bytes 12582916
  28.1 3.2 %collective-permute-start.11 = (bf16[96,2048]{1,0:T(8,128)(2,1)S(1)}, bf16[96,2048]{1,0:T(8,128)(2,1)S(1)}, u32[]{:S(2)}, u32[]{:S(2)}) collective-permute-start(bf16[96,2048]{1,0:T(8,128)(2,1)S(1)} %get-tuple-element.31), channel_id=1, source_target_pairs={{0,1},{1,0},{2,3},{3,2},{4,5},{5,4},{6,7},{7,6},{8,9},{9,8},{10,11... | collective-permute-start | bytes 1179656 | tf_op jit(solution)/shard_map/ppermute | solution.py:353
  28.7 1.5 %collective-permute-start.9 = (bf16[32,2048]{1,0:T(8,128)(2,1)S(1)}, bf16[32,2048]{1,0:T(8,128)(2,1)S(1)}, u32[]{:S(2)}, u32[]{:S(2)}) collective-permute-start(bf16[32,2048]{1,0:T(8,128)(2,1)S(1)} %get-tuple-element.29), channel_id=1, source_target_pairs={{0,1},{1,0},{2,3},{3,2},{4,5},{5,4},{6,7},{7,6},{8,9},{9,8},{10,11... | collective-permute-start | bytes 393224 | tf_op jit(solution)/shard_map/ppermute | solution.py:353
  30.3 12.2 %collective-permute-start.10 = (bf16[32,2048]{1,0:T(8,128)(2,1)S(1)}, bf16[32,2048]{1,0:T(8,128)(2,1)S(1)}, u32[]{:S(2)}, u32[]{:S(2)}) collective-permute-start(bf16[32,2048]{1,0:T(8,128)(2,1)S(1)} %shard_map.142), channel_id=1, source_target_pairs={{0,10},{1,9},{2,8},{3,11},{4,14},{5,13},{6,12},{7,15},{8,2},{9,1},... | collective-permute-start | bytes 393224 | tf_op jit(solution)/shard_map/ppermute | solution.py:350
  31.4 11.5 %collective-permute-start.12 = (bf16[32,2048]{1,0:T(8,128)(2,1)S(1)}, bf16[32,2048]{1,0:T(8,128)(2,1)S(1)}, u32[]{:S(2)}, u32[]{:S(2)}) collective-permute-start(bf16[32,2048]{1,0:T(8,128)(2,1)S(1)} %get-tuple-element.38), channel_id=1, source_target_pairs={{0,6},{1,5},{2,4},{3,7},{4,2},{5,1},{6,0},{7,3},{8,14},{9,13},{10,... | collective-permute-start | bytes 393224 | tf_op jit(solution)/shard_map/ppermute | solution.py:350
  34.7 8.3 %collective-permute-start.13 = (bf16[32,2048]{1,0:T(8,128)(2,1)S(1)}, bf16[32,2048]{1,0:T(8,128)(2,1)S(1)}, u32[]{:S(2)}, u32[]{:S(2)}) collective-permute-start(bf16[32,2048]{1,0:T(8,128)(2,1)S(1)} %get-tuple-element.39), channel_id=1, source_target_pairs={{0,12},{1,15},{2,14},{3,13},{4,8},{5,11},{6,10},{7,9},{8,4},{9,7},... | collective-permute-start | bytes 393224 | tf_op jit(solution)/shard_map/ppermute | solution.py:350
  35.8 7.2 %collective-permute-start.14 = (bf16[32,2048]{1,0:T(8,128)(2,1)S(1)}, bf16[32,2048]{1,0:T(8,128)(2,1)S(1)}, u32[]{:S(2)}, u32[]{:S(2)}) collective-permute-start(bf16[32,2048]{1,0:T(8,128)(2,1)S(1)} %get-tuple-element.32), channel_id=1, source_target_pairs={{1,3},{3,1},{5,7},{7,5},{9,11},{11,9},{13,15},{15,13},{17,19},{19,... | collective-permute-start | bytes 393224 | tf_op jit(solution)/shard_map/ppermute | solution.py:350
  43.0 1.3 %collective-permute-start.15 = (bf16[16,2048]{1,0:T(8,128)(2,1)S(1)}, bf16[16,2048]{1,0:T(8,128)(2,1)S(1)}, u32[]{:S(2)}, u32[]{:S(2)}) collective-permute-start(bf16[16,2048]{1,0:T(8,128)(2,1)S(1)} %slice.7), channel_id=1, source_target_pairs={{0,1},{1,0},{2,3},{3,2},{4,5},{5,4},{6,7},{7,6},{8,9},{9,8},{10,11... | collective-permute-start | bytes 196616 | tf_op jit(solution)/shard_map/ppermute | solution.py:353
